TPU v7x, 256 devices: a whole 4x4x8 slice. The times are simulated.
256 devices in a mesh: de: 128 (over x, z, y), ha: 2 (over core).
Axes of the slice: x: 4, y: 4, z: 8, core: 2. Of those that a mesh axis runs over, the one named last changes fastest.
Arguments:
- tokens: bfloat16 [16384, 2048], P('de'), may hold values from -6 to 6
- out_grad: bfloat16 [16384, 2048], P('de'), may hold values from -6 to 6
- router_logits: float32 [16384, 128], P('de'), may hold values from -2.5 to 302
- routes: int32 [16384, 8], P('de'), may hold values from 0 to 127, all different within a row; in each aligned block of 128 rows (0 to 127, 128 to 255, ...) at most 10 rows name the same one
- gate_weight: bfloat16 [128, 2048, 768], P('de', None, 'ha'), may hold values from -0.125 to 0.125
- up_weight: bfloat16 [128, 2048, 768], P('de', None, 'ha'), may hold values from -0.125 to 0.125
- down_weight: bfloat16 [128, 768, 2048], P('de', 'ha'), may hold values from -0.21875 to 0.21875
Outputs:
- input_grad: bfloat16 [16384, 2048], P('de')
- logit_grad: float32 [16384, 128], P('de')
- gate_weight_grad: bfloat16 [128, 2048, 768], P('de', None, 'ha')
- up_weight_grad: bfloat16 [128, 2048, 768], P('de', None, 'ha')
- down_weight_grad: bfloat16 [128, 768, 2048], P('de', 'ha')
Inputs may be any that keep to these rules, and one draw needn't show every extreme that they name: `routes`: each row names 8 different experts. Among the rows of one device at most 10 name any one expert, and in every draw the rows of some device name some expert exactly 10 times.
All inputs are finite; a program needn't handle non-finite values.
Results may differ from a plain program's by a relative error of at most 0.0071.
Values may be sent and summed in bfloat16 or wider, within the bound.
A program may use at most 128 MiB of HBM per device.

v0:
```python
import jax
import jax.numpy as jnp
from jax import lax
from jax.sharding import PartitionSpec as P

WIN = 2


def spread(value, axis, source):
    kept = jnp.where(lax.axis_index(axis) == source, value, 0).astype(value.dtype)
    return lax.psum(kept, axis)


def owner_pass(recv_tokens, recv_grads, recv_weight, w_gate, w_up, w_down):
    model_width = recv_tokens.shape[2]
    slot_total = recv_tokens.shape[0] * recv_tokens.shape[1]
    rows_in = recv_tokens.reshape(slot_total, model_width)
    grads_in = recv_grads.reshape(slot_total, model_width)
    weight_in = recv_weight.reshape(slot_total).astype(jnp.float32)
    pre_gate = jnp.dot(rows_in, w_gate, preferred_element_type=jnp.float32)
    pre_up = jnp.dot(rows_in, w_up, preferred_element_type=jnp.float32)
    sig_gate = jax.nn.sigmoid(pre_gate)
    silu_gate = pre_gate * sig_gate
    hidden_act = silu_gate * pre_up
    back_grad = lax.dot_general(
        grads_in, w_down, (((1,), (1,)), ((), ())), preferred_element_type=jnp.float32
    )
    row_dots = jnp.sum(hidden_act * back_grad, axis=-1)
    scaled_back = weight_in[:, None] * back_grad
    scaled_act = (weight_in[:, None] * hidden_act).astype(jnp.bfloat16)
    grad_gate = (scaled_back * pre_up * sig_gate * (1.0 + pre_gate * (1.0 - sig_gate))).astype(
        jnp.bfloat16
    )
    grad_up = (scaled_back * silu_gate).astype(jnp.bfloat16)
    sum_gate = lax.dot_general(
        rows_in, grad_gate, (((0,), (0,)), ((), ())), preferred_element_type=jnp.float32
    )
    sum_up = lax.dot_general(
        rows_in, grad_up, (((0,), (0,)), ((), ())), preferred_element_type=jnp.float32
    )
    sum_down = lax.dot_general(
        scaled_act, grads_in, (((0,), (0,)), ((), ())), preferred_element_type=jnp.float32
    )
    partial_input = lax.dot_general(
        grad_gate, w_gate, (((1,), (1,)), ((), ())), preferred_element_type=jnp.float32
    )
    partial_input = partial_input + lax.dot_general(
        grad_up, w_up, (((1,), (1,)), ((), ())), preferred_element_type=jnp.float32
    )
    return (partial_input, row_dots, sum_gate, sum_up, sum_down)


def per_device(tokens, out_grad, router_logits, routes, gate_weight, up_weight, down_weight):
    n_dev = lax.axis_size("de")
    tok_rows, model_width = tokens.shape
    route_count = routes.shape[1]
    experts = n_dev * gate_weight.shape[0]
    slot_count = max(2, 5 * tok_rows * route_count // (4 * experts))
    w_gate = gate_weight[0]
    w_up = up_weight[0]
    w_down = down_weight[0]
    router_probs = jax.nn.softmax(router_logits, axis=-1)
    stride = n_dev // WIN
    dense_cols = []
    for window in range(WIN):
        sent_gate, sent_up, sent_down = (
            spread(w_gate, "de", window * stride),
            spread(w_up, "de", window * stride),
            spread(w_down, "de", window * stride),
        )
        pre_gate = jnp.dot(tokens, sent_gate, preferred_element_type=jnp.float32)
        pre_up = jnp.dot(tokens, sent_up, preferred_element_type=jnp.float32)
        hidden_act = pre_gate * jax.nn.sigmoid(pre_gate) * pre_up
        back_grad = lax.dot_general(
            out_grad, sent_down, (((1,), (1,)), ((), ())), preferred_element_type=jnp.float32
        )
        dense_cols.append(jnp.sum(hidden_act * back_grad, axis=-1))
    dense_dots = lax.psum(jnp.stack(dense_cols, axis=1), "ha")
    route_total = tok_rows * route_count
    total_slots = experts * slot_count
    flat_expert = routes.reshape(-1)
    expert_ids = jnp.arange(experts, dtype=jnp.int32)
    onehot = (flat_expert[:, None] == expert_ids[None, :]).astype(jnp.int32)
    ranking = jnp.sum(jnp.cumsum(onehot, axis=0) * onehot, axis=1) - 1
    slot_of_route = flat_expert * slot_count + ranking
    route_of_slot = (
        jnp.full((total_slots,), route_total, jnp.int32)
        .at[slot_of_route]
        .set(jnp.arange(route_total, dtype=jnp.int32))
    )
    token_of_slot = route_of_slot // route_count
    route_weight = (
        jnp.take_along_axis(router_probs, routes, axis=1).astype(jnp.bfloat16).reshape(-1)
    )
    padded_tokens = jnp.concatenate([tokens, jnp.zeros((1, model_width), tokens.dtype)])
    padded_grads = jnp.concatenate([out_grad, jnp.zeros((1, model_width), out_grad.dtype)])
    padded_weight = jnp.concatenate([route_weight, jnp.zeros((1,), route_weight.dtype)])
    send_tokens = padded_tokens[token_of_slot].reshape(experts, slot_count, model_width)
    send_grads = padded_grads[token_of_slot].reshape(experts, slot_count, model_width)
    send_weight = padded_weight[route_of_slot].reshape(experts, slot_count)
    recv_tokens, recv_grads, recv_weight = (
        lax.all_to_all(send_tokens, "de", split_axis=0, concat_axis=0, tiled=True),
        lax.all_to_all(send_grads, "de", split_axis=0, concat_axis=0, tiled=True),
        lax.all_to_all(send_weight, "de", split_axis=0, concat_axis=0, tiled=True),
    )
    input_slot, dot_slot, sum_gate, sum_up, sum_down = owner_pass(
        recv_tokens, recv_grads, recv_weight, w_gate, w_up, w_down
    )
    dot_slot = lax.psum(dot_slot, "ha")
    input_half = lax.psum_scatter(
        input_slot.reshape(experts, slot_count, model_width).astype(jnp.bfloat16),
        "ha",
        scatter_dimension=2,
        tiled=True,
    )
    dot_back = dot_slot.astype(jnp.bfloat16).reshape(experts, slot_count)
    input_full = lax.all_gather(input_half, "ha", axis=2, tiled=True)
    back_input, back_dots = (
        lax.all_to_all(input_full, "de", split_axis=0, concat_axis=0, tiled=True),
        lax.all_to_all(dot_back, "de", split_axis=0, concat_axis=0, tiled=True),
    )
    route_input = back_input.reshape(total_slots, model_width)[slot_of_route].astype(jnp.float32)
    input_grad = jnp.sum(route_input.reshape(tok_rows, route_count, model_width), axis=1).astype(
        jnp.bfloat16
    )
    route_dots = (
        back_dots.reshape(total_slots)[slot_of_route]
        .astype(jnp.float32)
        .reshape(tok_rows, route_count)
    )
    dot_table = jnp.sum(
        jnp.where(routes[:, :, None] == expert_ids[None, None, :], route_dots[:, :, None], 0.0),
        axis=1,
    )
    for window in range(WIN):
        dot_table = jnp.where(
            expert_ids[None, :] == window * stride, dense_dots[:, window : window + 1], dot_table
        )
    logit_grad = router_probs * (
        dot_table - jnp.sum(router_probs * dot_table, axis=-1, keepdims=True)
    )
    return (
        input_grad,
        logit_grad,
        sum_gate.astype(jnp.bfloat16)[None],
        sum_up.astype(jnp.bfloat16)[None],
        sum_down.astype(jnp.bfloat16)[None],
    )


def solution(mesh):
    return jax.shard_map(
        per_device,
        mesh=mesh,
        in_specs=(
            P("de", None),
            P("de", None),
            P("de", None),
            P("de", None),
            P("de", None, "ha"),
            P("de", None, "ha"),
            P("de", "ha", None),
        ),
        out_specs=(
            P("de", None),
            P("de", None),
            P("de", None, "ha"),
            P("de", None, "ha"),
            P("de", "ha", None),
        ),
        check_vma=False,
    )
```

profile of v0, /device:TPU:2, one launch (start us, length us, event | category | flops | bytes accessed | tf_op | source)
XLA Modules:
  0.0 937.7 jit_solution(9674473107665566664)
XLA Ops:
  10.0 4.3 scatter_custom_fusion
  14.4 6.1 gather_fusion.2
  20.5 9.6 %reshape.141 = bf16[128,10,2048]{2,1,0:T(8,128)(2,1)} reshape(bf16[1280,2048]{1,0:T(8,128)(2,1)} %gather_fusion.2) | data formatting | bytes 10485760 | tf_op jit(solution)/shard_map/reshape | solution.py:98
  30.1 16.0 %all-to-all-start.2 = ((bf16[128,10,2048]{2,1,0:T(8,128)(2,1)}), bf16[128,10,2048]{2,1,0:T(8,128)(2,1)}, u32[]{:S(2)}, u32[]{:S(2)}) async-start(bf16[128,10,2048]{2,1,0:T(8,128)(2,1)} %reshape.141), calls=%async_computation.2 | async-start | bytes 16777216 | tf_op jit(solution)/shard_map/all_to_all | solution.py:102
  53.6 6.2 gather_fusion.1
  59.8 9.6 %reshape.139 = bf16[128,10,2048]{2,1,0:T(8,128)(2,1)} reshape(bf16[1280,2048]{1,0:T(8,128)(2,1)} %gather_fusion.1) | data formatting | bytes 10485760 | tf_op jit(solution)/shard_map/reshape | solution.py:99
  69.4 213.2 %all-to-all-done.2 = bf16[128,10,2048]{2,1,0:T(8,128)(2,1)} async-done(((bf16[128,10,2048]{2,1,0:T(8,128)(2,1)}), bf16[128,10,2048]{2,1,0:T(8,128)(2,1)}, u32[]{:S(2)}, u32[]{:S(2)}) %all-to-all-start.2) | async-done | bytes 5242912 | tf_op jit(solution)/shard_map/all_to_all | solution.py:102
  282.6 8.8 all-to-all-start.1
  292.0 233.2 %all-reduce.6.cloned.1.call-done = (bf16[2048,384]{1,0:T(8,128)(2,1)}, bf16[2048,384]{1,0:T(8,128)(2,1)}, bf16[384,2048]{1,0:T(8,128)(2,1)}, bf16[2048,384]{1,0:...) async-done(((bf16[2048,384]{1,0:T(8,128)(2,1)}, bf16[2048,384]{1,0:T(8,128)(2,1)}, bf16[384,2048]{1,0:T(8,128)(2,1)}, bf16[2048,384]{1,0:T(8,128)(2,1)}, ...) | async-done | bytes 9437200 | tf_op jit(solution)/shard_map/psum | solution.py:11
  532.2 9.9 %reshape.142 = bf16[1280,2048]{1,0:T(8,128)(2,1)} reshape(bf16[128,10,2048]{2,1,0:T(8,128)(2,1)} %all-to-all-done.2) | data formatting | bytes 10485760 | tf_op jit(solution)/shard_map/reshape | solution.py:17
  542.1 6.1 fusion.6
  548.2 3.7 fusion.9
  552.0 9.8 %reshape.140 = bf16[1280,2048]{1,0:T(8,128)(2,1)} reshape(bf16[128,10,2048]{2,1,0:T(8,128)(2,1)} %all-to-all-done.1) | data formatting | bytes 10485760 | tf_op jit(solution)/shard_map/reshape | solution.py:18
  561.8 7.7 multiply_reduce_fusion
  572.7 11.8 %all-to-all-start.4 = ((bf16[128,1,10]{2,1,0:T(2,128)(2,1)}), bf16[128,1,10]{2,1,0:T(2,128)(2,1)S(1)}, u32[]{:S(2)}, u32[]{:S(2)}) async-start(bf16[128,1,10]{2,1,0:T(2,128)(2,1)} %all_to_all.29), calls=%async_computation.5 | async-start | bytes 131072 | tf_op jit(solution)/shard_map/all_to_all | solution.py:120
  584.6 10.8 %all-to-all-done.4 = bf16[128,1,10]{2,1,0:T(2,128)(2,1)S(1)} async-done(((bf16[128,1,10]{2,1,0:T(2,128)(2,1)}), bf16[128,1,10]{2,1,0:T(2,128)(2,1)S(1)}, u32[]{:S(2)}, u32[]{:S(2)}) %all-to-all-start.4) | async-done | bytes 2592 | tf_op jit(solution)/shard_map/all_to_all | solution.py:120
  595.7 6.8 gather_fusion.4
  603.1 6.7 gather_fusion.5
  610.3 8.0 gather_fusion
  618.4 17.3 %all_to_all.35 = bf16[128,1,10]{2,1,0:T(2,128)(2,1)S(1)} all-to-all(bf16[128,1,10]{2,1,0:T(2,128)(2,1)S(1)} %all_to_all.28), channel_id=1, replica_groups=mesh['de'=128,'ha'=2] {'de'}, dimensions={0} | all-to-all | bytes 5120 | tf_op jit(solution)/shard_map/all_to_all | solution.py:104
  636.1 3.7 multiply_convert_fusion.1
  642.8 4.8 add_convert_fusion
  647.6 9.6 %convert_element_type.78 = bf16[128,10,2048]{2,1,0:T(8,128)(2,1)} reshape(bf16[1280,2048]{1,0:T(8,128)(2,1)} %add_convert_fusion) | data formatting | bytes 10485760 | tf_op jit(solution)/shard_map/convert_element_type | solution.py:111
  657.3 15.8 %reduce-scatter.2.cloned.1.call-done = bf16[128,10,1024]{2,1,0:T(8,128)(2,1)} async-done(((bf16[128,10,2048]{2,1,0:T(8,128)(2,1)}), bf16[128,10,1024]{2,1,0:T(8,128)(2,1)}) %reduce-scatter.2.cloned.1.call-update) | async-done | bytes 2621456 | tf_op jit(solution)/shard_map/reduce_scatter | solution.py:110
  673.2 28.3 %all-gather.2.cloned.1.call-done = bf16[128,10,2048]{2,1,0:T(8,128)(2,1)} async-done(((bf16[128,10,1024]{2,1,0:T(8,128)(2,1)}), bf16[128,10,2048]{2,1,0:T(8,128)(2,1)}) %all-gather.2.cloned.1.call-update) | async-done | bytes 5242896 | tf_op jit(solution)/shard_map/all_gather | solution.py:117
  701.4 14.5 %all-to-all-start.3 = ((bf16[128,10,2048]{2,1,0:T(8,128)(2,1)}), bf16[128,10,2048]{2,1,0:T(8,128)(2,1)}, u32[]{:S(2)}, u32[]{:S(2)}) async-start(bf16[128,10,2048]{2,1,0:T(8,128)(2,1)} %all-gather.2.cloned.1.call-done), calls=%async_computation.4 | async-start | bytes 16777216 | tf_op jit(solution)/shard_map/all_to_all | solution.py:119
  716.7 6.7 fusion
  723.4 4.0 fusion.1
  730.9 172.3 %all-to-all-done.3 = bf16[128,10,2048]{2,1,0:T(8,128)(2,1)} async-done(((bf16[128,10,2048]{2,1,0:T(8,128)(2,1)}), bf16[128,10,2048]{2,1,0:T(8,128)(2,1)}, u32[]{:S(2)}, u32[]{:S(2)}) %all-to-all-start.3) | async-done | bytes 5242912 | tf_op jit(solution)/shard_map/all_to_all | solution.py:119
  903.2 9.8 %reshape.143 = bf16[1280,2048]{1,0:T(8,128)(2,1)} reshape(bf16[128,10,2048]{2,1,0:T(8,128)(2,1)} %all-to-all-done.3) | data formatting | bytes 10485760 | tf_op jit(solution)/shard_map/reshape | solution.py:122
  913.1 12.0 %gather_fusion.3 = bf16[1024,2048]{1,0:T(8,128)(2,1)} fusion(bf16[1280,2048]{1,0:T(8,128)(2,1)} %reshape.143, s32[1024]{0:T(1024)S(1)} %broadcast_clamp_fusion), kind=kCustom, calls=%fused_computation.3 | custom fusion | bytes 8392704 | tf_op jit(solution)/shard_map/gather | solution.py:122
  925.0 5.9 bitcast_reduce_fusion
  (110 shorter events, 30.2 us)
Async XLA Ops:
  7.2 7.2 copy-start.6
  30.1 252.5 %all-to-all-start.2 = ((bf16[128,10,2048]{2,1,0:T(8,128)(2,1)}), bf16[128,10,2048]{2,1,0:T(8,128)(2,1)}, u32[]{:S(2)}, u32[]{:S(2)}) async-start(bf16[128,10,2048]{2,1,0:T(8,128)(2,1)} %reshape.141), calls=%async_computation.2 | async-start | bytes 16777216 | tf_op jit(solution)/shard_map/all_to_all | solution.py:102
  46.1 479.1 %all-reduce.6.cloned.1.call-start = ((), (), s32[]{:S(2)}) async-start(), calls=%async_computation.8 | async-start | bytes 18874368 | tf_op jit(solution)/shard_map/psum | solution.py:11
  46.2 3.5 copy-start
  46.2 3.5 copy-start.1
  52.5 1.0 copy-start.5
  69.4 222.0 %copy-start.15 = (s32[128,8]{0,1:T(8,128)S(1)}, s32[128,8]{0,1:T(8,128)}, u32[]{:S(2)}) copy-start(s32[128,8]{0,1:T(8,128)} %param.10) | copy-start | bytes 12292
  69.4 222.2 %copy-start.14 = (f32[128,128]{1,0:T(8,128)S(1)}, f32[128,128]{1,0:T(8,128)}, u32[]{:S(2)}) copy-start(f32[128,128]{1,0:T(8,128)} %param.9) | copy-start | bytes 196612
  282.6 269.3 %all-to-all-start.1 = ((bf16[128,10,2048]{2,1,0:T(8,128)(2,1)}), bf16[128,10,2048]{2,1,0:T(8,128)(2,1)}, u32[]{:S(2)}, u32[]{:S(2)}) async-start(bf16[128,10,2048]{2,1,0:T(8,128)(2,1)} %reshape.139), calls=%async_computation.1 | async-start | bytes 16777216 | tf_op jit(solution)/shard_map/all_to_all | solution.py:103
  525.2 2.1 copy-start.17
  527.3 1.4 copy-start.13
  527.9 1.5 copy-start.9
  529.3 1.5 copy-start.16
  530.1 1.5 copy-start.12
  542.1 6.1 copy-start.2
  542.1 6.1 copy-start.4
  572.7 22.6 %all-to-all-start.4 = ((bf16[128,1,10]{2,1,0:T(2,128)(2,1)}), bf16[128,1,10]{2,1,0:T(2,128)(2,1)S(1)}, u32[]{:S(2)}, u32[]{:S(2)}) async-start(bf16[128,1,10]{2,1,0:T(2,128)(2,1)} %all_to_all.29), calls=%async_computation.5 | async-start | bytes 131072 | tf_op jit(solution)/shard_map/all_to_all | solution.py:120
  584.5 88.6 %reduce-scatter.2.cloned.1.call-start = ((), (), s32[]{:S(2)}) async-start(), calls=%async_computation.6 | async-start | bytes 12582912 | tf_op jit(solution)/shard_map/reduce_scatter | solution.py:110
  639.8 3.0 copy-start.7
  639.8 3.0 copy-start.3
  657.2 44.2 %all-gather.2.cloned.1.call-start = ((), (), s32[]{:S(2)}) async-start(), calls=%async_computation.7 | async-start | bytes 12582912 | tf_op jit(solution)/shard_map/all_gather | solution.py:117
  673.1 43.5 %copy-start.8 = (bf16[1280,384]{0,1:T(8,128)(2,1)S(1)}, bf16[1280,384]{0,1:T(8,128)(2,1)}, u32[]{:S(2)}) copy-start(bf16[1280,384]{0,1:T(8,128)(2,1)} %copy-done.7) | copy-start | bytes 2949124
  701.4 22.0 %slice-start = ((s8[5242880]{0:T(1024)(128)(4,1)}), s8[1048576]{0:T(1024)(128)(4,1)S(1)}, s32[]{:S(2)}) async-start(s8[5242880]{0:T(1024)(128)(4,1)} %bitcast.95), calls=%async_computation.9 | async-start | bytes 2097152
  701.4 201.8 %all-to-all-start.3 = ((bf16[128,10,2048]{2,1,0:T(8,128)(2,1)}), bf16[128,10,2048]{2,1,0:T(8,128)(2,1)}, u32[]{:S(2)}, u32[]{:S(2)}) async-start(bf16[128,10,2048]{2,1,0:T(8,128)(2,1)} %all-gather.2.cloned.1.call-done), calls=%async_computation.4 | async-start | bytes 16777216 | tf_op jit(solution)/shard_map/all_to_all | solution.py:119
  716.7 6.7 slice-start.1
  716.7 10.8 %slice-start.2 = ((s8[5242880]{0:T(1024)(128)(4,1)}), s8[4194304]{0:T(1024)(128)(4,1)S(1)}, s32[]{:S(2)}) async-start(s8[5242880]{0:T(1024)(128)(4,1)} %bitcast.97), calls=%async_computation.11 | async-start | bytes 8388608
  723.4 4.1 slice-start.3
  723.4 4.1 copy-start.10
  723.4 4.1 copy-start.11
Sparse Core Ops, SparseCore 0:
  53.9 471.2 all-reduce.5
  657.4 15.7 reduce-scatter.1
  674.9 26.4 all-gather.1
where the time goes:
time: 946 us; the launch traced here: 938 us
  waiting for transfers between devices  674 us (71%)
  local copies, waits for them, and re-layouts  115 us (12%)
  starting transfers between devices  51.1 us (5%)
  matrix products  44.7 us (5%)
  blocking collectives  19.8 us (2%)
  other arithmetic  19.2 us (2%)
  between operations  14.4 us (2%)
    psum x1, waiting for transfers between devices, spread(): return lax.psum(kept, axis)  233 us
    all_to_all x1, waiting for transfers between devices, per_device(): lax.all_to_all(send_tokens, 'de', split_axis=0, concat_axis=0, tiled=True)  213 us
    all_to_all x1, waiting for transfers between devices, per_device(): lax.all_to_all(input_full, 'de', split_axis=0, concat_axis=0, tiled=True)  172 us
    all_gather x1, waiting for transfers between devices, per_device(): input_full = lax.all_gather(input_half, 'ha', axis=2, tiled=True)  28.3 us
  transfers between devices with their start and end apart: 7, of which 6 were waited for; matrix products, arithmetic and copies ran while one was open for 7% of the time, Pallas kernels for 0%

commit v1 on v0

--- a/solution.py
+++ b/solution.py
@@ -4,6 +4,7 @@
 from jax.sharding import PartitionSpec as P
 
 WIN = 2
+DOT_COLS = 128
 
 
 def spread(value, axis, source):
@@ -11,12 +12,7 @@
     return lax.psum(kept, axis)
 
 
-def owner_pass(recv_tokens, recv_grads, recv_weight, w_gate, w_up, w_down):
-    model_width = recv_tokens.shape[2]
-    slot_total = recv_tokens.shape[0] * recv_tokens.shape[1]
-    rows_in = recv_tokens.reshape(slot_total, model_width)
-    grads_in = recv_grads.reshape(slot_total, model_width)
-    weight_in = recv_weight.reshape(slot_total).astype(jnp.float32)
+def owner_pass(rows_in, grads_in, weight_in, w_gate, w_up, w_down):
     pre_gate = jnp.dot(rows_in, w_gate, preferred_element_type=jnp.float32)
     pre_up = jnp.dot(rows_in, w_up, preferred_element_type=jnp.float32)
     sig_gate = jax.nn.sigmoid(pre_gate)
@@ -52,10 +48,15 @@
 
 def per_device(tokens, out_grad, router_logits, routes, gate_weight, up_weight, down_weight):
     n_dev = lax.axis_size("de")
+    n_ha = lax.axis_size("ha")
+    core = lax.axis_index("ha")
     tok_rows, model_width = tokens.shape
     route_count = routes.shape[1]
     experts = n_dev * gate_weight.shape[0]
     slot_count = max(2, 5 * tok_rows * route_count // (4 * experts))
+    half = -(-slot_count // n_ha)
+    slot_count = half * n_ha
+    feat = model_width // n_ha
     w_gate = gate_weight[0]
     w_up = up_weight[0]
     w_down = down_weight[0]
@@ -88,46 +89,48 @@
         .at[slot_of_route]
         .set(jnp.arange(route_total, dtype=jnp.int32))
     )
-    token_of_slot = route_of_slot // route_count
+    my_routes = lax.dynamic_index_in_dim(
+        route_of_slot.reshape(experts, n_ha, half), core, axis=1, keepdims=False
+    )
+    my_tokens = my_routes // route_count
     route_weight = (
         jnp.take_along_axis(router_probs, routes, axis=1).astype(jnp.bfloat16).reshape(-1)
     )
     padded_tokens = jnp.concatenate([tokens, jnp.zeros((1, model_width), tokens.dtype)])
     padded_grads = jnp.concatenate([out_grad, jnp.zeros((1, model_width), out_grad.dtype)])
     padded_weight = jnp.concatenate([route_weight, jnp.zeros((1,), route_weight.dtype)])
-    send_tokens = padded_tokens[token_of_slot].reshape(experts, slot_count, model_width)
-    send_grads = padded_grads[token_of_slot].reshape(experts, slot_count, model_width)
-    send_weight = padded_weight[route_of_slot].reshape(experts, slot_count)
-    recv_tokens, recv_grads, recv_weight = (
-        lax.all_to_all(send_tokens, "de", split_axis=0, concat_axis=0, tiled=True),
-        lax.all_to_all(send_grads, "de", split_axis=0, concat_axis=0, tiled=True),
-        lax.all_to_all(send_weight, "de", split_axis=0, concat_axis=0, tiled=True),
-    )
+    send_xg = jnp.concatenate([padded_tokens[my_tokens], padded_grads[my_tokens]], axis=1)
+    send_weight = padded_weight[my_routes]
+    recv_xg = lax.all_to_all(send_xg, "de", split_axis=0, concat_axis=0, tiled=True)
+    recv_weight = lax.all_to_all(send_weight, "de", split_axis=0, concat_axis=0, tiled=True)
+    all_xg = lax.all_gather(recv_xg, "ha", axis=0, tiled=False)
+    all_weight = lax.all_gather(recv_weight, "ha", axis=0, tiled=False)
+    rows_in = all_xg[:, :, :half].reshape(-1, model_width)
+    grads_in = all_xg[:, :, half:].reshape(-1, model_width)
+    weight_in = all_weight.reshape(-1).astype(jnp.float32)
     input_slot, dot_slot, sum_gate, sum_up, sum_down = owner_pass(
-        recv_tokens, recv_grads, recv_weight, w_gate, w_up, w_down
+        rows_in, grads_in, weight_in, w_gate, w_up, w_down
     )
     dot_slot = lax.psum(dot_slot, "ha")
     input_half = lax.psum_scatter(
-        input_slot.reshape(experts, slot_count, model_width).astype(jnp.bfloat16),
+        input_slot.reshape(n_ha, n_dev, half, model_width).astype(jnp.bfloat16),
         "ha",
-        scatter_dimension=2,
+        scatter_dimension=3,
         tiled=True,
     )
-    dot_back = dot_slot.astype(jnp.bfloat16).reshape(experts, slot_count)
-    input_full = lax.all_gather(input_half, "ha", axis=2, tiled=True)
-    back_input, back_dots = (
-        lax.all_to_all(input_full, "de", split_axis=0, concat_axis=0, tiled=True),
-        lax.all_to_all(dot_back, "de", split_axis=0, concat_axis=0, tiled=True),
+    dot_back = jnp.broadcast_to(
+        dot_slot.astype(jnp.bfloat16).reshape(n_ha, n_dev, half, 1), (n_ha, n_dev, half, DOT_COLS)
     )
-    route_input = back_input.reshape(total_slots, model_width)[slot_of_route].astype(jnp.float32)
-    input_grad = jnp.sum(route_input.reshape(tok_rows, route_count, model_width), axis=1).astype(
+    ret = jnp.concatenate([input_half, dot_back], axis=3)
+    ret = jnp.transpose(ret, (1, 0, 2, 3)).reshape(n_dev, slot_count, feat + DOT_COLS)
+    back = lax.all_to_all(ret, "de", split_axis=0, concat_axis=0, tiled=True)
+    back = back.reshape(total_slots, feat + DOT_COLS)[slot_of_route]
+    route_input = back[:, :feat].astype(jnp.float32)
+    input_part = jnp.sum(route_input.reshape(tok_rows, route_count, feat), axis=1).astype(
         jnp.bfloat16
     )
-    route_dots = (
-        back_dots.reshape(total_slots)[slot_of_route]
-        .astype(jnp.float32)
-        .reshape(tok_rows, route_count)
-    )
+    input_grad = lax.all_gather(input_part, "ha", axis=1, tiled=True)
+    route_dots = back[:, feat].astype(jnp.float32).reshape(tok_rows, route_count)
     dot_table = jnp.sum(
         jnp.where(routes[:, :, None] == expert_ids[None, None, :], route_dots[:, :, None], 0.0),
         axis=1,

time: 946 us -> 700 us (0.74)
  waiting for transfers between devices: 674 us -> 248 us
  blocking collectives: 19.8 us -> 228 us
  starting transfers between devices: 51.1 us -> 12.5 us
    all_to_all x4 -> x1, waiting for transfers between devices: 396 us -> 94.1 us  [per_device(): back = lax.all_to_all(ret, 'de', split_axis=0, concat_axis=0, tiled=True)]
    all_to_all x0 -> x1, blocking collectives: none -> 202 us  [per_device(): lax.all_to_all(send_xg, 'de', split_axis=0, concat_axis=0, tiled=True)]
    psum x1, waiting for transfers between devices: 233 us -> 154 us  [spread(): return lax.psum(kept, axis)]
    all_to_all x4 -> x1, starting transfers between devices: 51 us -> 12.3 us  [per_device(): back = lax.all_to_all(ret, 'de', split_axis=0, concat_axis=0, tiled=True)]
    all_gather x1, waiting for transfers between devices: 28.3 us -> 0.02 us  [per_device(): all_xg = lax.all_gather(recv_xg, 'ha', axis=0, tiled=False)]
    reshape x6 -> x5, local copies, waits for them, and re-layouts: 48.9 us -> 29.4 us  [the longest x1 10.2 us: per_device(): grads_in = all_xg[:, :, half:].reshape(-1, model_width)]
    unnamed x45 -> x58, local copies, waits for them, and re-layouts: 3.77 us -> 22 us
    gather x5 -> x6, local copies, waits for them, and re-layouts: 39.1 us -> 22.3 us  [the longest x2 6.31 us: per_device(): padded_grads[my_tokens]]
  transfers between devices with their start and end apart: 7 -> 4, of which waited for: 6 -> 2; matrix products, arithmetic and copies ran while one was open for 7% -> 17% of each run, Pallas kernels for 0% -> 0%
where the time goes in v1:
time: 700 us; the launch traced here: 689 us
  waiting for transfers between devices  248 us (35%)
  blocking collectives  228 us (33%)
  local copies, waits for them, and re-layouts  115 us (16%)
  matrix products  41.4 us (6%)
  other arithmetic  27.6 us (4%)
  between operations  16.6 us (2%)
  starting transfers between devices  12.5 us (2%)
    all_to_all x1, blocking collectives, per_device(): lax.all_to_all(send_xg, 'de', split_axis=0, concat_axis=0, tiled=True)  202 us
    psum x1, waiting for transfers between devices, spread(): return lax.psum(kept, axis)  154 us
    all_to_all x1, waiting for transfers between devices, per_device(): back = lax.all_to_all(ret, 'de', split_axis=0, concat_axis=0, tiled=True)  94.1 us
    unnamed x58, local copies, waits for them, and re-layouts  22 us
    all_to_all x1, blocking collectives, per_device(): lax.all_to_all(send_weight, 'de', split_axis=0, concat_axis=0, tiled=True)  19.3 us
  transfers between devices with their start and end apart: 4, of which 2 were waited for; matrix products, arithmetic and copies ran while one was open for 17% of the time, Pallas kernels for 0%

profile of v1, /device:TPU:2, one launch (start us, length us, event | category | flops | bytes accessed | tf_op | source)
XLA Modules:
  0.0 689.1 jit_solution(17287838984287379657)
XLA Ops:
  10.8 4.3 scatter_custom_fusion
  15.8 3.4 gather_fusion.1
  23.2 3.4 gather_fusion.2
  26.7 2.9 reshape.262
  29.5 10.5 %pad_maximum_fusion = bf16[128,10,2048]{2,1,0:T(8,128)(2,1)} fusion(bf16[128,5,2048]{2,1,0:T(8,128)(2,1)} %reshape.262, bf16[128,5,2048]{2,1,0:T(8,128)(2,1)} %reshape.254), kind=kLoop, calls=%fused_computation.7 | loop fusion | flops 10485760 | bytes 10485760 | tf_op jit(solution)/shard_map/concatenate | solution.py:102
  40.0 201.9 %all_to_all.20 = bf16[128,10,2048]{2,1,0:T(8,128)(2,1)S(1)} all-to-all(bf16[128,10,2048]{2,1,0:T(8,128)(2,1)} %pad_maximum_fusion), channel_id=1, replica_groups=mesh['de'=128,'ha'=2] {'de'}, dimensions={0} | all-to-all | bytes 10485760 | tf_op jit(solution)/shard_map/all_to_all | solution.py:104
  241.9 5.2 copy.92
  247.2 3.4 bitcast_select_fusion.5
  254.9 6.7 gather_fusion.4
  262.0 4.3 gather_fusion
  266.6 19.3 %all_to_all.21 = bf16[128,1,5]{2,1,0:T(2,128)(2,1)S(1)} all-to-all(bf16[128,1,5]{2,1,0:T(2,128)(2,1)S(1)} %all_to_all.16), channel_id=1, replica_groups=mesh['de'=128,'ha'=2] {'de'}, dimensions={0} | all-to-all | bytes 2560 | tf_op jit(solution)/shard_map/all_to_all | solution.py:105
  288.6 10.3 %fusion.33 = (bf16[2,128,5,2048]{3,1,0,2:T(8,128)(2,1)}, bf16[2,128,5,2048]{3,1,0,2:T(8,128)(2,1)}) fusion(bf16[2,128,10,2048]{3,1,0,2:T(8,128)(2,1)} %bitcast.109), kind=kLoop, calls=%fused_computation.97 | loop fusion | bytes 20971520 | tf_op jit(solution)/shard_map/slice | solution.py:108
  298.9 9.0 %copy.99 = bf16[2,128,5,2048]{3,2,1,0:T(8,128)(2,1)} copy(bf16[2,128,5,2048]{3,1,0,2:T(8,128)(2,1)} %get-tuple-element.13) | data formatting | bytes 10485760
  308.0 10.0 %reshape.238 = bf16[1280,2048]{1,0:T(8,128)(2,1)} reshape(bf16[2,128,5,2048]{3,2,1,0:T(8,128)(2,1)} %copy.99) | data formatting | bytes 10485760 | tf_op jit(solution)/shard_map/reshape | solution.py:108
  318.0 9.0 %copy.98 = bf16[2,128,5,2048]{3,2,1,0:T(8,128)(2,1)} copy(bf16[2,128,5,2048]{3,1,0,2:T(8,128)(2,1)} %get-tuple-element.14) | data formatting | bytes 10485760
  327.0 10.2 %reshape.237 = bf16[1280,2048]{1,0:T(8,128)(2,1)} reshape(bf16[2,128,5,2048]{3,2,1,0:T(8,128)(2,1)} %copy.98) | data formatting | bytes 10485760 | tf_op jit(solution)/shard_map/reshape | solution.py:109
  337.2 5.0 fusion.10
  344.5 7.1 %multiply_convert_fusion.2 = (bf16[1280,384]{0,1:T(8,128)(2,1)S(1)}, f32[1280]{0:T(1024)S(1)}, bf16[1280,384]{0,1:T(8,128)(2,1)S(1)}, f32[1280,384]{0,1:T(8,128)}) fusion(f32[1280,384]{0,1:T(8,128)S(1)} %fusion.10, f32[1280,384]{0,1:T(8,128)S(1)} %fusion.12, f32[1280]{0:T(1024)S(1)} %reshape.243, bf16[1280,2048]{1,0:T(8,128)(2,1)} %reshape.238, ...), kind=kOutput, calls=%fused_computation.20 | convolution fusion | flops 2021620480 | bytes 14690304 | tf_op jit(solution)/shard_map/dot_general | solution.py:16
  351.6 3.0 fusion.5
  354.6 4.8 add_convert_fusion
  359.5 10.0 %convert_element_type.79 = bf16[2,128,5,2048]{3,2,1,0:T(8,128)(2,1)} reshape(bf16[1280,2048]{1,0:T(8,128)(2,1)} %add_convert_fusion) | data formatting | bytes 10485760 | tf_op jit(solution)/shard_map/convert_element_type | solution.py:116
  369.5 153.8 %all-reduce.6.cloned.1.call-done = (bf16[2048,384]{1,0:T(8,128)(2,1)}, bf16[2048,384]{1,0:T(8,128)(2,1)}, bf16[384,2048]{1,0:T(8,128)(2,1)}, bf16[2048,384]{1,0:...) async-done(((bf16[2048,384]{1,0:T(8,128)(2,1)}, bf16[2048,384]{1,0:T(8,128)(2,1)}, bf16[384,2048]{1,0:T(8,128)(2,1)}, bf16[2048,384]{1,0:T(8,128)(2,1)}, ...) | async-done | bytes 9437200 | tf_op jit(solution)/shard_map/psum | solution.py:12
  533.5 3.5 maximum_bitcast_fusion
  537.5 4.0 copy.96
  541.4 12.3 %all-to-all-start.2 = ((bf16[128,10,1152]{2,1,0:T(8,128)(2,1)}), bf16[128,10,1152]{2,1,0:T(8,128)(2,1)}, u32[]{:S(2)}, u32[]{:S(2)}) async-start(bf16[128,10,1152]{2,1,0:T(8,128)(2,1)} %copy.96), calls=%async_computation.3 | async-start | bytes 9437184 | tf_op jit(solution)/shard_map/all_to_all | solution.py:126
  553.9 6.7 fusion.1
  560.6 4.0 fusion
  564.7 3.4 fusion.2
  568.1 94.1 %all-to-all-done.2 = bf16[128,10,1152]{2,1,0:T(8,128)(2,1)} async-done(((bf16[128,10,1152]{2,1,0:T(8,128)(2,1)}), bf16[128,10,1152]{2,1,0:T(8,128)(2,1)}, u32[]{:S(2)}, u32[]{:S(2)}) %all-to-all-start.2) | async-done | bytes 2949152 | tf_op jit(solution)/shard_map/all_to_all | solution.py:126
  662.2 5.0 reshape.240
  667.2 5.4 gather_fusion.3
  673.8 3.0 fusion.3
  (131 shorter events, 33.4 us)
Async XLA Ops:
  8.0 280.6 %all-gather.4.cloned.1.call-start = ((), (), s32[]{:S(2)}) async-start(), calls=%async_computation.5 | async-start | bytes 15728640 | tf_op jit(solution)/shard_map/all_gather | solution.py:106
  8.8 0.9 copy-start.11
  9.8 6.0 copy-start.4
  247.1 276.2 %all-reduce.6.cloned.1.call-start = ((), (), s32[]{:S(2)}) async-start(), calls=%async_computation.6 | async-start | bytes 18874368 | tf_op jit(solution)/shard_map/psum | solution.py:12
  247.2 3.5 copy-start
  247.2 3.5 copy-start.1
  253.5 0.7 copy-start.17
  253.5 0.9 copy-start.7
  253.6 279.6 %reduce-scatter.2.cloned.1.call-start = ((), (), s32[]{:S(2)}) async-start(), calls=%async_computation.4 | async-start | bytes 12582912 | tf_op jit(solution)/shard_map/reduce_scatter | solution.py:115
  337.2 5.0 copy-start.2
  337.2 5.0 copy-start.8
  342.2 2.3 copy-start.20
  351.6 3.0 copy-start.13
  351.6 3.0 copy-start.15
  369.4 153.9 %copy-start.5 = (bf16[128,2048]{1,0:T(8,128)(2,1)S(1)}, bf16[128,2048]{1,0:T(8,128)(2,1)}, u32[]{:S(2)}) copy-start(bf16[128,2048]{1,0:T(8,128)(2,1)} %param.7) | copy-start | bytes 1572868
  523.3 2.2 copy-start.19
  525.4 1.0 copy-start.3
  525.5 1.6 copy-start.10
  526.1 1.6 copy-start.6
  527.6 1.4 copy-start.18
  528.3 1.5 copy-start.9
  541.4 12.4 %copy-start.16 = (bf16[1280,384]{0,1:T(8,128)(2,1)S(1)}, bf16[1280,384]{0,1:T(8,128)(2,1)}, u32[]{:S(2)}) copy-start(bf16[1280,384]{0,1:T(8,128)(2,1)} %copy-done.15) | copy-start | bytes 2949124
  541.4 19.1 %slice-start = ((s8[5242880]{0:T(1024)(128)(4,1)}), s8[1048576]{0:T(1024)(128)(4,1)S(1)}, s32[]{:S(2)}) async-start(s8[5242880]{0:T(1024)(128)(4,1)} %bitcast.110), calls=%async_computation.7 | async-start | bytes 2097152
  541.4 120.8 %all-to-all-start.2 = ((bf16[128,10,1152]{2,1,0:T(8,128)(2,1)}), bf16[128,10,1152]{2,1,0:T(8,128)(2,1)}, u32[]{:S(2)}, u32[]{:S(2)}) async-start(bf16[128,10,1152]{2,1,0:T(8,128)(2,1)} %copy.96), calls=%async_computation.3 | async-start | bytes 9437184 | tf_op jit(solution)/shard_map/all_to_all | solution.py:126
  553.8 6.8 slice-start.1
  553.8 6.7 copy-start.14
  553.8 10.8 %slice-start.2 = ((s8[5242880]{0:T(1024)(128)(4,1)}), s8[4194304]{0:T(1024)(128)(4,1)S(1)}, s32[]{:S(2)}) async-start(s8[5242880]{0:T(1024)(128)(4,1)} %bitcast.112), calls=%async_computation.9 | async-start | bytes 8388608
  560.6 4.1 slice-start.3
  560.6 4.0 copy-start.21
  560.6 4.0 copy-start.22
  672.7 4.3 copy-start.12
Sparse Core Ops, SparseCore 0:
  247.3 23.6 all-gather.3
  369.6 16.1 reduce-scatter.1
Sparse Core Ops, SparseCore 1:
  254.6 268.6 all-reduce.5

commit v2 on v1

--- a/solution.py
+++ b/solution.py
@@ -2,6 +2,7 @@
 import jax.numpy as jnp
 from jax import lax
 from jax.sharding import PartitionSpec as P
+
 
 WIN = 2
 DOT_COLS = 128
@@ -46,7 +47,7 @@
     return (partial_input, row_dots, sum_gate, sum_up, sum_down)
 
 
-def per_device(tokens, out_grad, router_logits, routes, gate_weight, up_weight, down_weight):
+def layer(tokens, out_grad, router_logits, routes, gate_weight, up_weight, down_weight):
     n_dev = lax.axis_size("de")
     n_ha = lax.axis_size("ha")
     core = lax.axis_index("ha")
@@ -99,14 +100,15 @@
     padded_tokens = jnp.concatenate([tokens, jnp.zeros((1, model_width), tokens.dtype)])
     padded_grads = jnp.concatenate([out_grad, jnp.zeros((1, model_width), out_grad.dtype)])
     padded_weight = jnp.concatenate([route_weight, jnp.zeros((1,), route_weight.dtype)])
-    send_xg = jnp.concatenate([padded_tokens[my_tokens], padded_grads[my_tokens]], axis=1)
+    send_x = padded_tokens[my_tokens]
+    send_g = padded_grads[my_tokens]
     send_weight = padded_weight[my_routes]
-    recv_xg = lax.all_to_all(send_xg, "de", split_axis=0, concat_axis=0, tiled=True)
+    recv_x = lax.all_to_all(send_x, "de", split_axis=0, concat_axis=0, tiled=True)
+    recv_g = lax.all_to_all(send_g, "de", split_axis=0, concat_axis=0, tiled=True)
     recv_weight = lax.all_to_all(send_weight, "de", split_axis=0, concat_axis=0, tiled=True)
-    all_xg = lax.all_gather(recv_xg, "ha", axis=0, tiled=False)
-    all_weight = lax.all_gather(recv_weight, "ha", axis=0, tiled=False)
-    rows_in = all_xg[:, :, :half].reshape(-1, model_width)
-    grads_in = all_xg[:, :, half:].reshape(-1, model_width)
+    rows_in = lax.all_gather(recv_x, "ha", axis=0, tiled=True).reshape(-1, model_width)
+    grads_in = lax.all_gather(recv_g, "ha", axis=0, tiled=True).reshape(-1, model_width)
+    all_weight = lax.all_gather(recv_weight, "ha", axis=0, tiled=True)
     weight_in = all_weight.reshape(-1).astype(jnp.float32)
     input_slot, dot_slot, sum_gate, sum_up, sum_down = owner_pass(
         rows_in, grads_in, weight_in, w_gate, w_up, w_down
@@ -153,7 +155,7 @@
 
 def solution(mesh):
     return jax.shard_map(
-        per_device,
+        layer,
         mesh=mesh,
         in_specs=(
             P("de", None),

time: 700 us -> 705 us (level)
  blocking collectives: 228 us -> 242 us
  other arithmetic: 27.6 us -> 17.1 us
    all_gather x0 -> x2, local copies, waits for them, and re-layouts: none -> 17.9 us  [the longest x1 8.97 us: layer(): lax.all_gather(recv_x, 'ha', axis=0, tiled=True).reshape(-1, model_width)]
    unnamed x58 -> x56, local copies, waits for them, and re-layouts: 22 us -> 5.37 us
    all_to_all x2 -> x3, blocking collectives: 221 us -> 235 us  [the longest x1 112 us: layer(): lax.all_to_all(send_g, 'de', split_axis=0, concat_axis=0, tiled=True)]
    concatenate x2 -> x1, other arithmetic: 10.5 us -> 0.01 us  [layer(): jnp.concatenate([route_weight, jnp.zeros((1,), route_weight.dtype)])]
    slice x1 -> x0, local copies, waits for them, and re-layouts: 10.3 us -> none  [per_device(): rows_in = all_xg[:, :, :half].reshape(-1, model_width)]
    reshape x5, local copies, waits for them, and re-layouts: 29.4 us -> 37.8 us  [the longest x1 18.5 us: layer(): lax.all_gather(recv_x, 'ha', axis=0, tiled=True).reshape(-1, model_width)]
  transfers between devices with their start and end apart: 4 -> 5, of which waited for: 2 -> 2; matrix products, arithmetic and copies ran while one was open for 17% -> 18% of each run, Pallas kernels for 0% -> 0%
where the time goes in v2:
time: 705 us; the launch traced here: 694 us
  waiting for transfers between devices  252 us (36%)
  blocking collectives  242 us (34%)
  local copies, waits for them, and re-layouts  114 us (16%)
  matrix products  39.8 us (6%)
  other arithmetic  17.1 us (2%)
  between operations  16.3 us (2%)
  starting transfers between devices  12.5 us (2%)
    psum x1, waiting for transfers between devices, spread(): return lax.psum(kept, axis)  158 us
    all_to_all x1, blocking collectives, layer(): lax.all_to_all(send_g, 'de', split_axis=0, concat_axis=0, tiled=True)  112 us
    all_to_all x1, blocking collectives, layer(): lax.all_to_all(send_x, 'de', split_axis=0, concat_axis=0, tiled=True)  104 us
    all_to_all x1, waiting for transfers between devices, layer(): back = lax.all_to_all(ret, 'de', split_axis=0, concat_axis=0, tiled=True)  94.1 us
    all_to_all x1, blocking collectives, layer(): lax.all_to_all(send_weight, 'de', split_axis=0, concat_axis=0, tiled=True)  19.2 us
    reshape x1, local copies, waits for them, and re-layouts, layer(): lax.all_gather(recv_x, 'ha', axis=0, tiled=True).reshape(-1, model_width)  18.5 us
  transfers between devices with their start and end apart: 5, of which 2 were waited for; matrix products, arithmetic and copies ran while one was open for 18% of the time, Pallas kernels for 0%

profile of v2, /device:TPU:2, one launch (start us, length us, event | category | flops | bytes accessed | tf_op | source)
XLA Modules:
  0.0 693.7 jit_solution(11033534091896107442)
XLA Ops:
  11.1 4.3 scatter_custom_fusion
  16.1 3.4 gather_fusion.1
  22.4 111.8 %all_to_all.28 = bf16[128,5,2048]{2,1,0:T(8,128)(2,1)S(1)} all-to-all(bf16[128,5,2048]{2,1,0:T(8,128)(2,1)} %reshape.253), channel_id=1, replica_groups=mesh['de'=128,'ha'=2] {'de'}, dimensions={0} | all-to-all | bytes 5242880 | tf_op jit(solution)/shard_map/all_to_all | solution.py:107
  134.1 3.3 copy.95
  138.5 3.4 gather_fusion.2
  144.8 104.2 %all_to_all.29 = bf16[128,5,2048]{2,1,0:T(8,128)(2,1)S(1)} all-to-all(bf16[128,5,2048]{2,1,0:T(8,128)(2,1)} %reshape.261), channel_id=1, replica_groups=mesh['de'=128,'ha'=2] {'de'}, dimensions={0} | all-to-all | bytes 5242880 | tf_op jit(solution)/shard_map/all_to_all | solution.py:106
  249.0 3.2 copy.97
  252.3 3.4 bitcast_select_fusion.5
  255.7 2.9 bitcast_select_fusion.1
  260.0 6.7 gather_fusion.4
  267.3 4.3 gather_fusion
  271.9 19.2 %all_to_all.30 = bf16[128,1,5]{2,1,0:T(2,128)(2,1)S(1)} all-to-all(bf16[128,1,5]{2,1,0:T(2,128)(2,1)S(1)} %all_to_all.23), channel_id=1, replica_groups=mesh['de'=128,'ha'=2] {'de'}, dimensions={0} | all-to-all | bytes 2560 | tf_op jit(solution)/shard_map/all_to_all | solution.py:108
  293.4 9.0 %copy.96 = bf16[256,5,2048]{2,1,0:T(8,128)(2,1)} copy(bf16[256,5,2048]{2,0,1:T(8,128)(2,1)} %all-gather.4.cloned.1.call-done) | data formatting | bytes 10485760 | tf_op jit(solution)/shard_map/all_gather | solution.py:110
  302.4 10.2 %reshape.236 = bf16[1280,2048]{1,0:T(8,128)(2,1)} reshape(bf16[256,5,2048]{2,1,0:T(8,128)(2,1)} %copy.96) | data formatting | bytes 10485760 | tf_op jit(solution)/shard_map/reshape | solution.py:110
  312.6 9.0 %copy.98 = bf16[256,5,2048]{2,1,0:T(8,128)(2,1)} copy(bf16[256,5,2048]{2,0,1:T(8,128)(2,1)} %all-gather.6.cloned.1.call-done) | data formatting | bytes 10485760 | tf_op jit(solution)/shard_map/all_gather | solution.py:109
  321.5 18.5 %reshape.237 = bf16[1280,2048]{1,0:T(8,128)(2,1)} reshape(bf16[256,5,2048]{2,1,0:T(8,128)(2,1)} %copy.98) | data formatting | bytes 10485760 | tf_op jit(solution)/shard_map/reshape | solution.py:109
  340.0 5.4 fusion.12
  347.9 4.8 multiply_convert_fusion.2
  352.7 2.9 fusion.5
  355.7 4.8 add_convert_fusion
  360.5 10.0 %convert_element_type.79 = bf16[2,128,5,2048]{3,2,1,0:T(8,128)(2,1)} reshape(bf16[1280,2048]{1,0:T(8,128)(2,1)} %add_convert_fusion) | data formatting | bytes 10485760 | tf_op jit(solution)/shard_map/convert_element_type | solution.py:118
  370.5 157.6 %all-reduce.6.cloned.1.call-done = (bf16[2048,384]{1,0:T(8,128)(2,1)}, bf16[2048,384]{1,0:T(8,128)(2,1)}, bf16[384,2048]{1,0:T(8,128)(2,1)}, bf16[2048,384]{1,0:...) async-done(((bf16[2048,384]{1,0:T(8,128)(2,1)}, bf16[2048,384]{1,0:T(8,128)(2,1)}, bf16[384,2048]{1,0:T(8,128)(2,1)}, bf16[2048,384]{1,0:T(8,128)(2,1)}, ...) | async-done | bytes 9437200 | tf_op jit(solution)/shard_map/psum | solution.py:13
  538.4 3.5 maximum_bitcast_fusion
  542.3 4.0 copy.100
  546.3 12.3 %all-to-all-start.3 = ((bf16[128,10,1152]{2,1,0:T(8,128)(2,1)}), bf16[128,10,1152]{2,1,0:T(8,128)(2,1)}, u32[]{:S(2)}, u32[]{:S(2)}) async-start(bf16[128,10,1152]{2,1,0:T(8,128)(2,1)} %copy.100), calls=%async_computation.4 | async-start | bytes 9437184 | tf_op jit(solution)/shard_map/all_to_all | solution.py:128
  558.7 6.7 fusion
  565.5 4.0 fusion.1
  569.5 3.4 fusion.2
  573.0 94.1 %all-to-all-done.3 = bf16[128,10,1152]{2,1,0:T(8,128)(2,1)} async-done(((bf16[128,10,1152]{2,1,0:T(8,128)(2,1)}), bf16[128,10,1152]{2,1,0:T(8,128)(2,1)}, u32[]{:S(2)}, u32[]{:S(2)}) %all-to-all-start.3) | async-done | bytes 2949152 | tf_op jit(solution)/shard_map/all_to_all | solution.py:128
  667.1 5.0 reshape.239
  672.1 5.4 gather_fusion.3
  678.6 3.0 fusion.3
  (134 shorter events, 33.6 us)
Async XLA Ops:
  8.0 285.4 %all-gather.4.cloned.1.call-start = ((), (), s32[]{:S(2)}) async-start(), calls=%async_computation.5 | async-start | bytes 7864320 | tf_op jit(solution)/shard_map/all_gather | solution.py:110
  9.5 0.6 copy-start.11
  10.2 5.8 copy-start.3
  137.4 1.0 copy-start.5
  137.4 175.1 %all-gather.6.cloned.1.call-start = ((), (), s32[]{:S(2)}) async-start(), calls=%async_computation.6 | async-start | bytes 7864320 | tf_op jit(solution)/shard_map/all_gather | solution.py:109
  252.2 275.9 %all-reduce.6.cloned.1.call-start = ((), (), s32[]{:S(2)}) async-start(), calls=%async_computation.8 | async-start | bytes 18874368 | tf_op jit(solution)/shard_map/psum | solution.py:13
  252.3 3.5 copy-start
  252.3 3.5 copy-start.1
  258.6 0.7 copy-start.17
  258.6 0.9 copy-start.8
  258.6 279.4 %reduce-scatter.2.cloned.1.call-start = ((), (), s32[]{:S(2)}) async-start(), calls=%async_computation.7 | async-start | bytes 12582912 | tf_op jit(solution)/shard_map/reduce_scatter | solution.py:117
  340.0 5.5 copy-start.2
  347.9 4.8 copy-start.20
  352.7 3.0 copy-start.15
  352.7 3.0 copy-start.13
  370.5 157.7 %copy-start.6 = (bf16[128,2048]{1,0:T(8,128)(2,1)S(1)}, bf16[128,2048]{1,0:T(8,128)(2,1)}, u32[]{:S(2)}) copy-start(bf16[128,2048]{1,0:T(8,128)(2,1)} %param.7) | copy-start | bytes 1572868
  528.1 2.2 copy-start.19
  530.3 1.0 copy-start.4
  530.3 1.6 copy-start.10
  530.9 1.6 copy-start.7
  532.5 1.4 copy-start.18
  533.1 1.5 copy-start.9
  546.3 12.4 %copy-start.16 = (bf16[1280,384]{0,1:T(8,128)(2,1)S(1)}, bf16[1280,384]{0,1:T(8,128)(2,1)}, u32[]{:S(2)}) copy-start(bf16[1280,384]{0,1:T(8,128)(2,1)} %copy-done.15) | copy-start | bytes 2949124
  546.3 19.1 %slice-start.2 = ((s8[5242880]{0:T(1024)(128)(4,1)}), s8[1048576]{0:T(1024)(128)(4,1)S(1)}, s32[]{:S(2)}) async-start(s8[5242880]{0:T(1024)(128)(4,1)} %bitcast.111), calls=%async_computation.11 | async-start | bytes 2097152
  546.3 120.8 %all-to-all-start.3 = ((bf16[128,10,1152]{2,1,0:T(8,128)(2,1)}), bf16[128,10,1152]{2,1,0:T(8,128)(2,1)}, u32[]{:S(2)}, u32[]{:S(2)}) async-start(bf16[128,10,1152]{2,1,0:T(8,128)(2,1)} %copy.100), calls=%async_computation.4 | async-start | bytes 9437184 | tf_op jit(solution)/shard_map/all_to_all | solution.py:128
  558.7 6.8 slice-start.3
  558.7 6.7 copy-start.14
  558.7 10.8 %slice-start = ((s8[5242880]{0:T(1024)(128)(4,1)}), s8[4194304]{0:T(1024)(128)(4,1)S(1)}, s32[]{:S(2)}) async-start(s8[5242880]{0:T(1024)(128)(4,1)} %bitcast.109), calls=%async_computation.9 | async-start | bytes 8388608
  565.5 4.1 slice-start.1
  565.5 4.1 copy-start.21
  565.5 4.0 copy-start.22
  677.5 4.3 copy-start.12
Sparse Core Ops, SparseCore 0:
  137.5 16.2 all-gather.3
  252.3 16.1 all-gather.5
  370.7 16.0 reduce-scatter.1
Sparse Core Ops, SparseCore 1:
  259.7 268.4 all-reduce.5

commit v3 on v2

--- a/solution.py
+++ b/solution.py
@@ -11,6 +11,13 @@
 def spread(value, axis, source):
     kept = jnp.where(lax.axis_index(axis) == source, value, 0).astype(value.dtype)
     return lax.psum(kept, axis)
+
+
+def share_halves(mine, core, n_ha):
+    other = lax.ppermute(mine, "ha", [(i, (i + 1) % n_ha) for i in range(n_ha)])
+    full = jnp.zeros((n_ha,) + mine.shape, mine.dtype)
+    full = lax.dynamic_update_index_in_dim(full, mine, core, 0)
+    return lax.dynamic_update_index_in_dim(full, other, 1 - core, 0)
 
 
 def owner_pass(rows_in, grads_in, weight_in, w_gate, w_up, w_down):
@@ -106,9 +113,9 @@
     recv_x = lax.all_to_all(send_x, "de", split_axis=0, concat_axis=0, tiled=True)
     recv_g = lax.all_to_all(send_g, "de", split_axis=0, concat_axis=0, tiled=True)
     recv_weight = lax.all_to_all(send_weight, "de", split_axis=0, concat_axis=0, tiled=True)
-    rows_in = lax.all_gather(recv_x, "ha", axis=0, tiled=True).reshape(-1, model_width)
-    grads_in = lax.all_gather(recv_g, "ha", axis=0, tiled=True).reshape(-1, model_width)
-    all_weight = lax.all_gather(recv_weight, "ha", axis=0, tiled=True)
+    rows_in = share_halves(recv_x, core, n_ha).reshape(-1, model_width)
+    grads_in = share_halves(recv_g, core, n_ha).reshape(-1, model_width)
+    all_weight = share_halves(recv_weight, core, n_ha)
     weight_in = all_weight.reshape(-1).astype(jnp.float32)
     input_slot, dot_slot, sum_gate, sum_up, sum_down = owner_pass(
         rows_in, grads_in, weight_in, w_gate, w_up, w_down

time: 705 us -> 670 us (0.950)
  blocking collectives: 242 us -> 4.69 us
  waiting for transfers between devices: 252 us -> 413 us
  starting transfers between devices: 12.5 us -> 49.9 us
    all_to_all x3 -> x0, blocking collectives: 235 us -> none  [the longest x1 112 us: layer(): lax.all_to_all(send_g, 'de', split_axis=0, concat_axis=0, tiled=True)]
    all_to_all x0 -> x3, waiting for transfers between devices: none -> 216 us  [the longest x1 115 us: layer(): lax.all_to_all(send_g, 'de', split_axis=0, concat_axis=0, tiled=True)]
    psum x1, waiting for transfers between devices: 158 us -> 102 us  [spread(): return lax.psum(kept, axis)]
    all_to_all x0 -> x3, starting transfers between devices: none -> 36.8 us  [the longest x1 16.1 us: layer(): lax.all_to_all(send_x, 'de', split_axis=0, concat_axis=0, tiled=True)]
    dynamic_update_slice x0 -> x5, local copies, waits for them, and re-layouts: none -> 18.4 us  [the longest x3 9.55 us: share_halves(): full = lax.dynamic_update_index_in_dim(full, mine, core, 0)]
    all_gather x2 -> x0, local copies, waits for them, and re-layouts: 17.9 us -> none  [the longest x1 8.97 us: layer(): lax.all_gather(recv_x, 'ha', axis=0, tiled=True).reshape(-1, model_width)]
    another operation x3 -> x5, local copies, waits for them, and re-layouts: 0.11 us -> 8.71 us
    reshape x2, local copies, waits for them, and re-layouts: 28.6 us -> 20.2 us  [the longest x1 10.2 us: layer(): grads_in = share_halves(recv_g, core, n_ha).reshape(-1, model_width)]
  transfers between devices with their start and end apart: 5 -> 9, of which waited for: 2 -> 6; matrix products, arithmetic and copies ran while one was open for 18% -> 20% of each run, Pallas kernels for 0% -> 0%
where the time goes in v3:
time: 670 us; the launch traced here: 658 us
  waiting for transfers between devices  413 us (62%)
  local copies, waits for them, and re-layouts  119 us (18%)
  starting transfers between devices  49.9 us (7%)
  matrix products  37.6 us (6%)
  other arithmetic  17.1 us (3%)
  between operations  16.7 us (2%)
    all_to_all x1, waiting for transfers between devices, layer(): lax.all_to_all(send_g, 'de', split_axis=0, concat_axis=0, tiled=True)  115 us
    psum x1, waiting for transfers between devices, spread(): return lax.psum(kept, axis)  102 us
    all_to_all x1, waiting for transfers between devices, layer(): back = lax.all_to_all(ret, 'de', split_axis=0, concat_axis=0, tiled=True)  94.1 us
    all_to_all x1, waiting for transfers between devices, layer(): lax.all_to_all(send_x, 'de', split_axis=0, concat_axis=0, tiled=True)  89.5 us
    all_to_all x1, starting transfers between devices, layer(): lax.all_to_all(send_x, 'de', split_axis=0, concat_axis=0, tiled=True)  16.1 us
  transfers between devices with their start and end apart: 9, of which 6 were waited for; matrix products, arithmetic and copies ran while one was open for 20% of the time, Pallas kernels for 0%

profile of v3, /device:TPU:2, one launch (start us, length us, event | category | flops | bytes accessed | tf_op | source)
XLA Modules:
  0.0 658.1 jit_solution(6659702816181287465)
XLA Ops:
  11.1 4.3 scatter_custom_fusion
  16.1 3.4 gather_fusion.2
  22.4 16.1 %all-to-all-start.2 = ((bf16[128,5,2048]{2,1,0:T(8,128)(2,1)}), bf16[128,5,2048]{2,1,0:T(8,128)(2,1)}, u32[]{:S(2)}, u32[]{:S(2)}) async-start(bf16[128,5,2048]{2,1,0:T(8,128)(2,1)} %reshape.262), calls=%async_computation.2 | async-start | bytes 8388608 | tf_op jit(solution)/shard_map/all_to_all | solution.py:113
  38.6 3.4 gather_fusion.1
  44.9 89.5 %all-to-all-done.2 = bf16[128,5,2048]{2,1,0:T(8,128)(2,1)} async-done(((bf16[128,5,2048]{2,1,0:T(8,128)(2,1)}), bf16[128,5,2048]{2,1,0:T(8,128)(2,1)}, u32[]{:S(2)}, u32[]{:S(2)}) %all-to-all-start.2) | async-done | bytes 2621472 | tf_op jit(solution)/shard_map/all_to_all | solution.py:113
  134.5 8.8 %all-to-all-start.1 = ((bf16[128,5,2048]{2,1,0:T(8,128)(2,1)}), bf16[128,5,2048]{2,1,0:T(8,128)(2,1)}, u32[]{:S(2)}, u32[]{:S(2)}) async-start(bf16[128,5,2048]{2,1,0:T(8,128)(2,1)} %reshape.254), calls=%async_computation.1 | async-start | bytes 8388608 | tf_op jit(solution)/shard_map/all_to_all | solution.py:114
  149.7 5.4 copy.103
  155.2 115.3 %all-to-all-done.1 = bf16[128,5,2048]{2,1,0:T(8,128)(2,1)} async-done(((bf16[128,5,2048]{2,1,0:T(8,128)(2,1)}), bf16[128,5,2048]{2,1,0:T(8,128)(2,1)}, u32[]{:S(2)}, u32[]{:S(2)}) %all-to-all-start.1) | async-done | bytes 2621472 | tf_op jit(solution)/shard_map/all_to_all | solution.py:114
  270.6 5.6 copy.101
  276.8 6.7 %gather_fusion.4 = bf16[1024]{0:T(1024)(128)(2,1)S(1)} fusion(f32[128,128]{1,0:T(8,128)S(1)} %fusion.28, s32[1024]{0:T(1024)S(1)} %reshape.277), kind=kCustom, calls=%fused_computation.4 | custom fusion | bytes 12288 | tf_op jit(solution)/shard_map/jit(take_along_axis)/gather | solution.py:105
  284.2 4.3 gather_fusion
  289.4 11.9 %all-to-all-start = ((bf16[128,1,5]{2,1,0:T(2,128)(2,1)}), bf16[128,1,5]{2,1,0:T(2,128)(2,1)S(1)}, u32[]{:S(2)}, u32[]{:S(2)}) async-start(bf16[128,1,5]{2,1,0:T(2,128)(2,1)} %all_to_all.23), calls=%async_computation | async-start | bytes 131072 | tf_op jit(solution)/shard_map/all_to_all | solution.py:115
  301.4 10.9 %all-to-all-done = bf16[128,1,5]{2,1,0:T(2,128)(2,1)S(1)} async-done(((bf16[128,1,5]{2,1,0:T(2,128)(2,1)}), bf16[128,1,5]{2,1,0:T(2,128)(2,1)S(1)}, u32[]{:S(2)}, u32[]{:S(2)}) %all-to-all-start) | async-done | bytes 1312 | tf_op jit(solution)/shard_map/all_to_all | solution.py:115
  314.3 4.3 broadcast.175.clone
  318.6 4.8 bitcast_dynamic-update-slice_fusion
  323.4 4.3 broadcast.175.clone.1
  327.7 4.8 bitcast_dynamic-update-slice_fusion.1
  332.5 8.9 %copy_dynamic-update-slice_fusion = (bf16[2,128,5,2048]{3,2,1,0:T(8,128)(2,1)}, bf16[2,128,5,2048]{3,2,1,0:T(8,128)(2,1)}) fusion(bf16[2,128,5,2048]{3,2,1,0:T(8,128)(2,1)} %bitcast_dynamic-update-slice_fusion, s32[]{:T(128)S(6)} %select_n.120, bf16[1,128,5,2048]{3,1,2,0:T(8,128)(2,1)} %bitcast.14, ...), kind=kLoop, calls=%fused_computation.10 | loop fusion | bytes 13631492 | tf_op jit(solution)/shard_map/jit(dynamic_update_index_in_dim)/dynamic_update_slice | solution.py:20
  341.3 10.0 %reshape.238 = bf16[1280,2048]{1,0:T(8,128)(2,1)} reshape(bf16[2,128,5,2048]{3,2,1,0:T(8,128)(2,1)} %get-tuple-element.26) | data formatting | bytes 10485760 | tf_op jit(solution)/shard_map/reshape | solution.py:116
  351.4 10.2 %reshape.237 = bf16[1280,2048]{1,0:T(8,128)(2,1)} reshape(bf16[2,128,5,2048]{3,2,1,0:T(8,128)(2,1)} %get-tuple-element.27) | data formatting | bytes 10485760 | tf_op jit(solution)/shard_map/reshape | solution.py:117
  361.6 5.0 fusion.7
  375.2 4.9 add_convert_fusion
  380.1 10.0 %convert_element_type.79 = bf16[2,128,5,2048]{3,2,1,0:T(8,128)(2,1)} reshape(bf16[1280,2048]{1,0:T(8,128)(2,1)} %add_convert_fusion) | data formatting | bytes 10485760 | tf_op jit(solution)/shard_map/convert_element_type | solution.py:125
  390.1 102.2 %all-reduce.6.cloned.1.call-done = (bf16[2048,384]{1,0:T(8,128)(2,1)}, bf16[2048,384]{1,0:T(8,128)(2,1)}, bf16[384,2048]{1,0:T(8,128)(2,1)}, bf16[2048,384]{1,0:...) async-done(((bf16[2048,384]{1,0:T(8,128)(2,1)}, bf16[2048,384]{1,0:T(8,128)(2,1)}, bf16[384,2048]{1,0:T(8,128)(2,1)}, bf16[2048,384]{1,0:T(8,128)(2,1)}, ...) | async-done | bytes 9437200 | tf_op jit(solution)/shard_map/psum | solution.py:13
  502.5 3.5 maximum_bitcast_fusion
  506.5 4.0 copy.106
  510.5 12.3 %all-to-all-start.3 = ((bf16[128,10,1152]{2,1,0:T(8,128)(2,1)}), bf16[128,10,1152]{2,1,0:T(8,128)(2,1)}, u32[]{:S(2)}, u32[]{:S(2)}) async-start(bf16[128,10,1152]{2,1,0:T(8,128)(2,1)} %copy.106), calls=%async_computation.4 | async-start | bytes 9437184 | tf_op jit(solution)/shard_map/all_to_all | solution.py:135
  522.9 6.7 %fusion = bf16[1,2048,384]{2,1,0:T(8,128)(2,1)} fusion(bf16[1280,2048]{1,0:T(8,128)(2,1)} %reshape.238, bf16[1280,384]{0,1:T(8,128)(2,1)S(1)} %copy-done.17), kind=kOutput, calls=%fused_computation.15 | convolution fusion | flops 2014052352 | bytes 7798784 | tf_op jit(solution)/shard_map/dot_general | solution.py:39
  529.6 4.0 fusion.1
  537.1 94.1 %all-to-all-done.3 = bf16[128,10,1152]{2,1,0:T(8,128)(2,1)} async-done(((bf16[128,10,1152]{2,1,0:T(8,128)(2,1)}), bf16[128,10,1152]{2,1,0:T(8,128)(2,1)}, u32[]{:S(2)}, u32[]{:S(2)}) %all-to-all-start.3) | async-done | bytes 2949152 | tf_op jit(solution)/shard_map/all_to_all | solution.py:135
  631.3 5.0 reshape.240
  636.3 5.4 gather_fusion.3
  (152 shorter events, 51.5 us)
Async XLA Ops:
  10.2 5.9 copy-start.5
  22.4 16.1 %copy-start.3 = (bf16[128,2048]{1,0:T(8,128)(2,1)S(1)}, bf16[128,2048]{1,0:T(8,128)(2,1)}, u32[]{:S(2)}) copy-start(bf16[128,2048]{1,0:T(8,128)(2,1)} %param.8) | copy-start | bytes 1572868
  22.4 112.0 %all-to-all-start.2 = ((bf16[128,5,2048]{2,1,0:T(8,128)(2,1)}), bf16[128,5,2048]{2,1,0:T(8,128)(2,1)}, u32[]{:S(2)}, u32[]{:S(2)}) async-start(bf16[128,5,2048]{2,1,0:T(8,128)(2,1)} %reshape.262), calls=%async_computation.2 | async-start | bytes 8388608 | tf_op jit(solution)/shard_map/all_to_all | solution.py:113
  134.5 136.1 %all-to-all-start.1 = ((bf16[128,5,2048]{2,1,0:T(8,128)(2,1)}), bf16[128,5,2048]{2,1,0:T(8,128)(2,1)}, u32[]{:S(2)}, u32[]{:S(2)}) async-start(bf16[128,5,2048]{2,1,0:T(8,128)(2,1)} %reshape.254), calls=%async_computation.1 | async-start | bytes 8388608 | tf_op jit(solution)/shard_map/all_to_all | solution.py:114
  143.2 349.1 %all-reduce.6.cloned.1.call-start = ((), (), s32[]{:S(2)}) async-start(), calls=%async_computation.6 | async-start | bytes 18874368 | tf_op jit(solution)/shard_map/psum | solution.py:13
  143.3 3.4 copy-start
  143.3 3.4 copy-start.1
  155.0 121.1 %copy-start.18 = (s32[128,8]{0,1:T(8,128)S(1)}, s32[128,8]{0,1:T(8,128)}, u32[]{:S(2)}) copy-start(s32[128,8]{0,1:T(8,128)} %param.10) | copy-start | bytes 12292
  155.0 121.3 %copy-start.8 = (f32[128,128]{1,0:T(8,128)S(1)}, f32[128,128]{1,0:T(8,128)}, u32[]{:S(2)}) copy-start(f32[128,128]{1,0:T(8,128)} %param.9) | copy-start | bytes 196612
  155.0 177.4 %collective-permute-start.2 = (bf16[128,5,2048]{2,0,1:T(8,128)(2,1)}, bf16[128,5,2048]{2,0,1:T(8,128)(2,1)}, u32[]{:S(2)}, u32[]{:S(2)}) collective-permute-start(bf16[128,5,2048]{2,0,1:T(8,128)(2,1)} %copy.103), channel_id=1, source_target_pairs={{0,1},{1,0},{2,3},{3,2},{4,5},{5,4},{6,7},{7,6},{8,9},{9,8},{10,11... | collective-permute-start | bytes 7864328 | tf_op jit(solution)/shard_map/ppermute | solution.py:17
  276.2 56.3 %collective-permute-start.1 = (bf16[128,5,2048]{2,0,1:T(8,128)(2,1)}, bf16[128,5,2048]{2,0,1:T(8,128)(2,1)}, u32[]{:S(2)}, u32[]{:S(2)}) collective-permute-start(bf16[128,5,2048]{2,0,1:T(8,128)(2,1)} %copy.101), channel_id=1, source_target_pairs={{0,1},{1,0},{2,3},{3,2},{4,5},{5,4},{6,7},{7,6},{8,9},{9,8},{10,11... | collective-permute-start | bytes 7864328 | tf_op jit(solution)/shard_map/ppermute | solution.py:17
  289.4 22.9 %all-to-all-start = ((bf16[128,1,5]{2,1,0:T(2,128)(2,1)}), bf16[128,1,5]{2,1,0:T(2,128)(2,1)S(1)}, u32[]{:S(2)}, u32[]{:S(2)}) async-start(bf16[128,1,5]{2,1,0:T(2,128)(2,1)} %all_to_all.23), calls=%async_computation | async-start | bytes 131072 | tf_op jit(solution)/shard_map/all_to_all | solution.py:115
  301.3 200.9 %reduce-scatter.2.cloned.1.call-start = ((), (), s32[]{:S(2)}) async-start(), calls=%async_computation.5 | async-start | bytes 12582912 | tf_op jit(solution)/shard_map/reduce_scatter | solution.py:124
  312.3 1.6 collective-permute-start
  361.6 5.0 copy-start.2
  361.6 7.5 %slice-start = ((s8[5242880]{0:T(1024)(128)(4,1)}), s8[4194304]{0:T(1024)(128)(4,1)S(1)}, s32[]{:S(2)}) async-start(s8[5242880]{0:T(1024)(128)(4,1)} %bitcast.116), calls=%async_computation.7 | async-start | bytes 8388608
  366.6 2.5 slice-start.1
  366.6 2.5 copy-start.9
  369.2 3.1 copy-start.23
  372.2 3.0 copy-start.16
  372.2 3.0 copy-start.14
  390.1 102.3 %copy-start.6 = (bf16[128,2048]{1,0:T(8,128)(2,1)S(1)}, bf16[128,2048]{1,0:T(8,128)(2,1)}, u32[]{:S(2)}) copy-start(bf16[128,2048]{1,0:T(8,128)(2,1)} %param.7) | copy-start | bytes 1572868
  510.5 12.4 %copy-start.17 = (bf16[1280,384]{0,1:T(8,128)(2,1)S(1)}, bf16[1280,384]{0,1:T(8,128)(2,1)}, u32[]{:S(2)}) copy-start(bf16[1280,384]{0,1:T(8,128)(2,1)} %copy-done.16) | copy-start | bytes 2949124
  510.5 19.1 %slice-start.4 = ((s8[5242880]{0:T(1024)(128)(4,1)}), s8[1048576]{0:T(1024)(128)(4,1)S(1)}, s32[]{:S(2)}) async-start(s8[5242880]{0:T(1024)(128)(4,1)} %bitcast.120), calls=%async_computation.11 | async-start | bytes 2097152
  510.5 120.8 %all-to-all-start.3 = ((bf16[128,10,1152]{2,1,0:T(8,128)(2,1)}), bf16[128,10,1152]{2,1,0:T(8,128)(2,1)}, u32[]{:S(2)}, u32[]{:S(2)}) async-start(bf16[128,10,1152]{2,1,0:T(8,128)(2,1)} %copy.106), calls=%async_computation.4 | async-start | bytes 9437184 | tf_op jit(solution)/shard_map/all_to_all | solution.py:135
  522.8 6.8 %slice-start.5 = ((s8[5242880]{0:T(1024)(128)(4,1)}), s8[4194304]{0:T(1024)(128)(4,1)S(1)}, s32[]{:S(2)}) async-start(s8[5242880]{0:T(1024)(128)(4,1)} %bitcast.120), calls=%async_computation.12 | async-start | bytes 8388608
  522.9 6.8 %copy-start.15 = (bf16[1280,384]{0,1:T(8,128)(2,1)S(1)}, bf16[1280,384]{0,1:T(8,128)(2,1)}, u32[]{:S(2)}) copy-start(bf16[1280,384]{0,1:T(8,128)(2,1)} %copy-done.14) | copy-start | bytes 2949124
  522.9 10.8 %slice-start.2 = ((s8[5242880]{0:T(1024)(128)(4,1)}), s8[4194304]{0:T(1024)(128)(4,1)S(1)}, s32[]{:S(2)}) async-start(s8[5242880]{0:T(1024)(128)(4,1)} %bitcast.118), calls=%async_computation.9 | async-start | bytes 8388608
  529.6 4.1 slice-start.3
  529.6 4.1 copy-start.22
  529.6 4.0 copy-start.24
  641.7 4.3 copy-start.13
  (8 other events, 12.4 us)
Sparse Core Ops, SparseCore 0:
  151.0 341.2 all-reduce.5
Sparse Core Ops, SparseCore 1:
  390.2 15.8 reduce-scatter.1

commit v4 on v3

--- a/solution.py
+++ b/solution.py
@@ -107,16 +107,17 @@
     padded_tokens = jnp.concatenate([tokens, jnp.zeros((1, model_width), tokens.dtype)])
     padded_grads = jnp.concatenate([out_grad, jnp.zeros((1, model_width), out_grad.dtype)])
     padded_weight = jnp.concatenate([route_weight, jnp.zeros((1,), route_weight.dtype)])
-    send_x = padded_tokens[my_tokens]
-    send_g = padded_grads[my_tokens]
-    send_weight = padded_weight[my_routes]
-    recv_x = lax.all_to_all(send_x, "de", split_axis=0, concat_axis=0, tiled=True)
-    recv_g = lax.all_to_all(send_g, "de", split_axis=0, concat_axis=0, tiled=True)
-    recv_weight = lax.all_to_all(send_weight, "de", split_axis=0, concat_axis=0, tiled=True)
-    rows_in = share_halves(recv_x, core, n_ha).reshape(-1, model_width)
-    grads_in = share_halves(recv_g, core, n_ha).reshape(-1, model_width)
-    all_weight = share_halves(recv_weight, core, n_ha)
-    weight_in = all_weight.reshape(-1).astype(jnp.float32)
+    send_weight = jnp.broadcast_to(
+        padded_weight[my_routes][:, :, None], my_routes.shape + (DOT_COLS,)
+    )
+    send_xg = jnp.concatenate(
+        [padded_tokens[my_tokens], padded_grads[my_tokens], send_weight], axis=2
+    )
+    recv_xg = lax.all_to_all(send_xg, "de", split_axis=0, concat_axis=0, tiled=True)
+    all_xg = share_halves(recv_xg, core, n_ha).reshape(-1, 2 * model_width + DOT_COLS)
+    rows_in = all_xg[:, :model_width]
+    grads_in = all_xg[:, model_width : 2 * model_width]
+    weight_in = all_xg[:, 2 * model_width].astype(jnp.float32)
     input_slot, dot_slot, sum_gate, sum_up, sum_down = owner_pass(
         rows_in, grads_in, weight_in, w_gate, w_up, w_down
     )

time: 670 us -> 712 us (1.063)
  blocking collectives: 4.69 us -> 213 us
  waiting for transfers between devices: 413 us -> 285 us
  starting transfers between devices: 49.9 us -> 12.5 us
  local copies, waits for them, and re-layouts: 119 us -> 107 us
    all_to_all x3 -> x0, waiting for transfers between devices: 216 us -> none  [the longest x1 115 us: layer(): lax.all_to_all(send_g, 'de', split_axis=0, concat_axis=0, tiled=True)]
    all_to_all x0 -> x1, blocking collectives: none -> 209 us  [layer(): lax.all_to_all(send_xg, 'de', split_axis=0, concat_axis=0, tiled=True)]
    psum x1, waiting for transfers between devices: 102 us -> 196 us  [spread(): return lax.psum(kept, axis)]
    all_to_all x3 -> x0, starting transfers between devices: 36.8 us -> none  [the longest x1 16.1 us: layer(): lax.all_to_all(send_x, 'de', split_axis=0, concat_axis=0, tiled=True)]
    another operation x5 -> x3, local copies, waits for them, and re-layouts: 8.71 us -> 0.11 us
    all_to_all x4 -> x1, local copies, waits for them, and re-layouts: 11.9 us -> 3.46 us  [layer(): lax.all_to_all(send_xg, 'de', split_axis=0, concat_axis=0, tiled=True)]
    reshape x2 -> x1, local copies, waits for them, and re-layouts: 20.2 us -> 17.3 us  [layer(): share_halves(recv_xg, core, n_ha).reshape(-1, 2 * model_width + DOT_COLS)]
    gather x5 -> x6, local copies, waits for them, and re-layouts: 16.9 us -> 17.1 us  [the longest x2 6.27 us: layer(): padded_grads[my_tokens]]
  transfers between devices with their start and end apart: 9 -> 4, of which waited for: 6 -> 2; matrix products, arithmetic and copies ran while one was open for 20% -> 14% of each run, Pallas kernels for 0% -> 0%
where the time goes in v4:
time: 712 us; the launch traced here: 700 us
  waiting for transfers between devices  285 us (40%)
  blocking collectives  213 us (30%)
  local copies, waits for them, and re-layouts  107 us (15%)
  matrix products  42.6 us (6%)
  other arithmetic  23.9 us (3%)
  between operations  16.3 us (2%)
  starting transfers between devices  12.5 us (2%)
    all_to_all x1, blocking collectives, layer(): lax.all_to_all(send_xg, 'de', split_axis=0, concat_axis=0, tiled=True)  209 us
    psum x1, waiting for transfers between devices, spread(): return lax.psum(kept, axis)  196 us
    all_to_all x1, waiting for transfers between devices, layer(): back = lax.all_to_all(ret, 'de', split_axis=0, concat_axis=0, tiled=True)  89 us
    reshape x1, local copies, waits for them, and re-layouts, layer(): share_halves(recv_xg, core, n_ha).reshape(-1, 2 * model_width + DOT_COLS)  17.3 us
  transfers between devices with their start and end apart: 4, of which 2 were waited for; matrix products, arithmetic and copies ran while one was open for 14% of the time, Pallas kernels for 0%

profile of v4, /device:TPU:2, one launch (start us, length us, event | category | flops | bytes accessed | tf_op | source)
XLA Modules:
  0.0 700.3 jit_solution(8229776382096614171)
XLA Ops:
  11.5 4.3 scatter_custom_fusion
  17.4 6.7 gather_fusion.4
  24.6 4.3 gather_fusion.2
  29.4 3.4 gather_fusion
  32.8 2.8 reshape.232
  36.8 3.4 gather_fusion.1
  40.2 2.8 reshape.240
  43.2 4.7 pad_maximum_fusion
  48.0 208.6 %all_to_all.10 = bf16[128,5,4224]{2,1,0:T(8,128)(2,1)S(1)} all-to-all(bf16[128,5,4224]{2,1,0:T(8,128)(2,1)S(1)} %pad_maximum_fusion), channel_id=1, replica_groups=mesh['de'=128,'ha'=2] {'de'}, dimensions={0} | all-to-all | bytes 10813440 | tf_op jit(solution)/shard_map/all_to_all | solution.py:116
  256.6 3.5 copy.64
  261.6 3.4 bitcast_select_fusion.5
  265.0 2.9 bitcast_select_fusion.1
  268.2 6.2 broadcast_in_dim.108
  274.3 8.0 %bitcast_dynamic-update-slice_fusion = bf16[2,128,5,4224]{3,2,1,0:T(8,128)(2,1)} fusion(bf16[2,128,5,4224]{3,2,1,0:T(8,128)(2,1)} %broadcast_in_dim.108, s32[]{:T(128)S(6)} %select_n.111, bf16[128,5,4224]{2,1,0:T(8,128)(2,1)} %copy-done), kind=kLoop, calls=%fused_computation.8 | loop fusion | bytes 17301508 | tf_op jit(solution)/shard_map/jit(dynamic_update_index_in_dim)/dynamic_update_slice | solution.py:19
  282.4 9.1 %copy_dynamic-update-slice_fusion = bf16[2,128,5,4224]{3,2,1,0:T(8,128)(2,1)} fusion(bf16[2,128,5,4224]{3,2,1,0:T(8,128)(2,1)} %bitcast_dynamic-update-slice_fusion, s32[]{:T(128)S(6)} %select_n.117, bf16[1,128,5,4224]{3,1,2,0:T(8,128)(2,1)} %bitcast.8), kind=kLoop, calls=%fused_computation.9 | loop fusion | bytes 14057476 | tf_op jit(solution)/shard_map/jit(dynamic_update_index_in_dim)/dynamic_update_slice | solution.py:20
  291.5 17.3 %reshape.224 = bf16[1280,4224]{1,0:T(8,128)(2,1)} reshape(bf16[2,128,5,4224]{3,2,1,0:T(8,128)(2,1)} %copy_dynamic-update-slice_fusion) | data formatting | bytes 21626880 | tf_op jit(solution)/shard_map/reshape | solution.py:117
  310.1 5.0 fusion.10
  317.7 2.9 multiply_convert_fusion.2
  320.6 2.9 fusion.32
  323.6 4.8 add_convert_fusion
  328.4 10.2 %convert_element_type.69 = bf16[2,128,5,2048]{3,2,1,0:T(8,128)(2,1)} reshape(bf16[1280,2048]{1,0:T(8,128)(2,1)} %add_convert_fusion) | data formatting | bytes 10485760 | tf_op jit(solution)/shard_map/convert_element_type | solution.py:126
  338.6 196.1 %all-reduce.6.cloned.1.call-done = (bf16[2048,384]{1,0:T(8,128)(2,1)}, bf16[2048,384]{1,0:T(8,128)(2,1)}, bf16[384,2048]{1,0:T(8,128)(2,1)}, bf16[2048,384]{1,0:...) async-done(((bf16[2048,384]{1,0:T(8,128)(2,1)}, bf16[2048,384]{1,0:T(8,128)(2,1)}, bf16[384,2048]{1,0:T(8,128)(2,1)}, bf16[2048,384]{1,0:T(8,128)(2,1)}, ...) | async-done | bytes 9437200 | tf_op jit(solution)/shard_map/psum | solution.py:13
  545.0 3.5 maximum_bitcast_fusion
  548.9 4.0 copy.67
  552.9 12.3 %all-to-all-start.1 = ((bf16[128,10,1152]{2,1,0:T(8,128)(2,1)}), bf16[128,10,1152]{2,1,0:T(8,128)(2,1)}, u32[]{:S(2)}, u32[]{:S(2)}) async-start(bf16[128,10,1152]{2,1,0:T(8,128)(2,1)} %copy.67), calls=%async_computation.2 | async-start | bytes 9437184 | tf_op jit(solution)/shard_map/all_to_all | solution.py:136
  565.2 6.7 fusion.24
  571.9 6.7 fusion.27
  578.6 6.0 fusion.21
  584.6 89.0 %all-to-all-done.1 = bf16[128,10,1152]{2,1,0:T(8,128)(2,1)} async-done(((bf16[128,10,1152]{2,1,0:T(8,128)(2,1)}), bf16[128,10,1152]{2,1,0:T(8,128)(2,1)}, u32[]{:S(2)}, u32[]{:S(2)}) %all-to-all-start.1) | async-done | bytes 2949152 | tf_op jit(solution)/shard_map/all_to_all | solution.py:136
  673.6 5.0 reshape.226
  678.6 5.5 gather_fusion.3
  685.2 3.0 fusion.30
  (135 shorter events, 28.9 us)
Async XLA Ops:
  8.0 526.8 %all-reduce.6.cloned.1.call-start = ((), (), s32[]{:S(2)}) async-start(), calls=%async_computation.4 | async-start | bytes 18874368 | tf_op jit(solution)/shard_map/psum | solution.py:13
  8.8 1.6 copy-start.12
  10.5 5.9 copy-start.7
  17.4 6.9 copy-start.18
  24.6 4.8 copy-start.4
  256.6 5.0 copy-start
  261.6 20.8 %collective-permute-start = (bf16[128,5,4224]{2,0,1:T(8,128)(2,1)}, bf16[128,5,4224]{2,0,1:T(8,128)(2,1)}, u32[]{:S(2)}, u32[]{:S(2)}) collective-permute-start(bf16[128,5,4224]{2,0,1:T(8,128)(2,1)} %copy.64), channel_id=1, source_target_pairs={{0,1},{1,0},{2,3},{3,2},{4,5},{5,4},{6,7},{7,6},{8,9},{9,8},{10,11... | collective-permute-start | bytes 16220168 | tf_op jit(solution)/shard_map/ppermute | solution.py:17
  261.6 3.4 copy-start.1
  261.6 3.4 copy-start.2
  268.0 276.7 %reduce-scatter.2.cloned.1.call-start = ((), (), s32[]{:S(2)}) async-start(), calls=%async_computation.3 | async-start | bytes 12582912 | tf_op jit(solution)/shard_map/reduce_scatter | solution.py:125
  308.8 6.3 slice-start
  310.1 5.0 slice-start.1
  310.1 5.1 slice-start.2
  315.2 2.4 copy-start.25
  315.2 2.4 copy-start.9
  317.7 3.0 copy-start.27
  320.6 3.0 copy-start.14
  320.6 3.0 copy-start.16
  338.6 196.2 %copy-start.5 = (bf16[128,2048]{1,0:T(8,128)(2,1)S(1)}, bf16[128,2048]{1,0:T(8,128)(2,1)}, u32[]{:S(2)}) copy-start(bf16[128,2048]{1,0:T(8,128)(2,1)} %param.7) | copy-start | bytes 1572868
  534.8 2.2 copy-start.24
  536.9 1.6 copy-start.11
  537.5 1.6 copy-start.6
  539.7 1.5 copy-start.10
  552.9 12.3 %copy-start.17 = (bf16[1280,384]{0,1:T(8,128)(2,1)S(1)}, bf16[1280,384]{0,1:T(8,128)(2,1)}, u32[]{:S(2)}) copy-start(bf16[1280,384]{0,1:T(8,128)(2,1)} %copy-done.16) | copy-start | bytes 2949124
  552.9 120.7 %all-to-all-start.1 = ((bf16[128,10,1152]{2,1,0:T(8,128)(2,1)}), bf16[128,10,1152]{2,1,0:T(8,128)(2,1)}, u32[]{:S(2)}, u32[]{:S(2)}) async-start(bf16[128,10,1152]{2,1,0:T(8,128)(2,1)} %copy.67), calls=%async_computation.2 | async-start | bytes 9437184 | tf_op jit(solution)/shard_map/all_to_all | solution.py:136
  565.2 6.7 copy-start.15
  571.9 6.7 copy-start.26
  571.9 6.7 copy-start.28
  684.1 4.3 copy-start.13
  684.1 4.6 copy-start.8
  684.1 4.6 copy-start.20
  684.1 4.6 copy-start.22
  (4 other events, 3.6 us)
Sparse Core Ops, SparseCore 0:
  268.1 266.6 all-reduce.5
Sparse Core Ops, SparseCore 1:
  338.7 17.0 reduce-scatter.1

commit v5 on v4

--- a/solution.py
+++ b/solution.py
@@ -15,9 +15,9 @@
 
 def share_halves(mine, core, n_ha):
     other = lax.ppermute(mine, "ha", [(i, (i + 1) % n_ha) for i in range(n_ha)])
-    full = jnp.zeros((n_ha,) + mine.shape, mine.dtype)
-    full = lax.dynamic_update_index_in_dim(full, mine, core, 0)
-    return lax.dynamic_update_index_in_dim(full, other, 1 - core, 0)
+    first = jnp.where(core == 0, mine, other)
+    second = jnp.where(core == 0, other, mine)
+    return jnp.stack([first, second])
 
 
 def owner_pass(rows_in, grads_in, weight_in, w_gate, w_up, w_down):

time: 712 us -> 711 us (level)
  local copies, waits for them, and re-layouts: 107 us -> 82.7 us
  other arithmetic: 23.9 us -> 40.4 us
    dynamic_update_slice x2 -> x0, local copies, waits for them, and re-layouts: 17.1 us -> none  [the longest x1 9.12 us: share_halves(): return lax.dynamic_update_index_in_dim(full, other, 1 - core, 0)]
    another operation x3 -> x5, other arithmetic: 0.27 us -> 16.8 us  [the longest x2 16.5 us: share_halves(): return jnp.stack([first, second])]
  transfers between devices with their start and end apart: 4 -> 4, of which waited for: 2 -> 3; matrix products, arithmetic and copies ran while one was open for 14% -> 13% of each run, Pallas kernels for 0% -> 0%
where the time goes in v5:
time: 711 us; the launch traced here: 700 us
  waiting for transfers between devices  292 us (41%)
  blocking collectives  213 us (30%)
  local copies, waits for them, and re-layouts  82.7 us (12%)
  matrix products  42.7 us (6%)
  other arithmetic  40.4 us (6%)
  between operations  16.4 us (2%)
  starting transfers between devices  12.8 us (2%)
    all_to_all x1, blocking collectives, layer(): lax.all_to_all(send_xg, 'de', split_axis=0, concat_axis=0, tiled=True)  209 us
    psum x1, waiting for transfers between devices, spread(): return lax.psum(kept, axis)  201 us
    all_to_all x1, waiting for transfers between devices, layer(): back = lax.all_to_all(ret, 'de', split_axis=0, concat_axis=0, tiled=True)  89 us
    reshape x1, local copies, waits for them, and re-layouts, layer(): share_halves(recv_xg, core, n_ha).reshape(-1, 2 * model_width + DOT_COLS)  17.3 us
    another operation x2, other arithmetic, share_halves(): return jnp.stack([first, second])  16.5 us
  transfers between devices with their start and end apart: 4, of which 3 were waited for; matrix products, arithmetic and copies ran while one was open for 13% of the time, Pallas kernels for 0%

profile of v5, /device:TPU:2, one launch (start us, length us, event | category | flops | bytes accessed | tf_op | source)
XLA Modules:
  0.0 700.3 jit_solution(13314700394746682327)
XLA Ops:
  11.5 4.3 scatter_custom_fusion
  17.4 6.7 gather_fusion.4
  24.6 4.3 gather_fusion.2
  29.4 3.4 gather_fusion
  32.8 2.8 reshape.232
  36.8 3.4 gather_fusion.1
  40.2 2.8 reshape.240
  43.2 4.7 pad_maximum_fusion.1
  48.0 208.6 %all_to_all.10 = bf16[128,5,4224]{2,1,0:T(8,128)(2,1)S(1)} all-to-all(bf16[128,5,4224]{2,1,0:T(8,128)(2,1)S(1)} %pad_maximum_fusion.1), channel_id=1, replica_groups=mesh['de'=128,'ha'=2] {'de'}, dimensions={0} | all-to-all | bytes 10813440 | tf_op jit(solution)/shard_map/all_to_all | solution.py:116
  256.6 3.5 copy.66
  261.5 3.5 bitcast_select_fusion.5
  265.0 2.9 bitcast_select_fusion.1
  270.7 7.9 %fusion = (bf16[1,128,5,4224]{3,2,1,0:T(8,128)(2,1)S(1)}, bf16[1,128,5,4224]{3,2,1,0:T(8,128)(2,1)S(1)}) fusion(bf16[128,5,4224]{2,1,0:T(8,128)(2,1)} %copy-done, bf16[128,5,4224]{2,0,1:T(8,128)(2,1)} %collective-permute-done, pred[]{:T(512)S(6)} %eq.74), kind=kLoop, calls=%fused_computation.10 | loop fusion | flops 5406720 | bytes 21626880 | tf_op jit(solution)/shard_map/stack | solution.py:20
  278.7 8.6 %pad_maximum_fusion = bf16[2,128,5,4224]{3,2,1,0:T(8,128)(2,1)} fusion(bf16[1,128,5,4224]{3,2,1,0:T(8,128)(2,1)S(1)} %get-tuple-element.14, bf16[1,128,5,4224]{3,2,1,0:T(8,128)(2,1)S(1)} %get-tuple-element.13), kind=kLoop, calls=%fused_computation.6 | loop fusion | flops 5406720 | bytes 21626880 | tf_op jit(solution)/shard_map/stack | solution.py:20
  287.3 17.3 %reshape.224 = bf16[1280,4224]{1,0:T(8,128)(2,1)} reshape(bf16[2,128,5,4224]{3,2,1,0:T(8,128)(2,1)} %pad_maximum_fusion) | data formatting | bytes 21626880 | tf_op jit(solution)/shard_map/reshape | solution.py:117
  305.9 5.0 fusion.10
  313.4 2.9 multiply_convert_fusion.2
  316.3 2.9 fusion.34
  319.3 5.0 add_convert_fusion
  324.3 9.8 %convert_element_type.69 = bf16[2,128,5,2048]{3,2,1,0:T(8,128)(2,1)} reshape(bf16[1280,2048]{1,0:T(8,128)(2,1)} %add_convert_fusion) | data formatting | bytes 10485760 | tf_op jit(solution)/shard_map/convert_element_type | solution.py:126
  334.1 200.6 %all-reduce.6.cloned.1.call-done = (bf16[2048,384]{1,0:T(8,128)(2,1)}, bf16[2048,384]{1,0:T(8,128)(2,1)}, bf16[384,2048]{1,0:T(8,128)(2,1)}, bf16[2048,384]{1,0:...) async-done(((bf16[2048,384]{1,0:T(8,128)(2,1)}, bf16[2048,384]{1,0:T(8,128)(2,1)}, bf16[384,2048]{1,0:T(8,128)(2,1)}, bf16[2048,384]{1,0:T(8,128)(2,1)}, ...) | async-done | bytes 9437200 | tf_op jit(solution)/shard_map/psum | solution.py:13
  541.8 2.5 all-reduce.2
  544.9 3.5 maximum_bitcast_fusion
  548.9 4.0 copy.70
  552.8 12.3 %all-to-all-start.1 = ((bf16[128,10,1152]{2,1,0:T(8,128)(2,1)}), bf16[128,10,1152]{2,1,0:T(8,128)(2,1)}, u32[]{:S(2)}, u32[]{:S(2)}) async-start(bf16[128,10,1152]{2,1,0:T(8,128)(2,1)} %copy.70), calls=%async_computation.2 | async-start | bytes 9437184 | tf_op jit(solution)/shard_map/all_to_all | solution.py:136
  565.2 6.7 fusion.26
  571.8 6.7 fusion.29
  578.6 6.0 fusion.23
  584.5 89.0 %all-to-all-done.1 = bf16[128,10,1152]{2,1,0:T(8,128)(2,1)} async-done(((bf16[128,10,1152]{2,1,0:T(8,128)(2,1)}), bf16[128,10,1152]{2,1,0:T(8,128)(2,1)}, u32[]{:S(2)}, u32[]{:S(2)}) %all-to-all-start.1) | async-done | bytes 2949152 | tf_op jit(solution)/shard_map/all_to_all | solution.py:136
  673.6 5.0 reshape.226
  678.6 5.4 gather_fusion.3
  685.2 3.0 fusion.32
  (134 shorter events, 28.9 us)
Async XLA Ops:
  8.0 526.7 %all-reduce.6.cloned.1.call-start = ((), (), s32[]{:S(2)}) async-start(), calls=%async_computation.4 | async-start | bytes 18874368 | tf_op jit(solution)/shard_map/psum | solution.py:13
  8.8 1.6 copy-start.12
  10.5 5.9 copy-start.7
  17.4 6.9 copy-start.18
  24.6 4.8 copy-start.4
  256.6 4.9 copy-start
  261.5 9.2 %collective-permute-start = (bf16[128,5,4224]{2,0,1:T(8,128)(2,1)}, bf16[128,5,4224]{2,0,1:T(8,128)(2,1)}, u32[]{:S(2)}, u32[]{:S(2)}) collective-permute-start(bf16[128,5,4224]{2,0,1:T(8,128)(2,1)} %copy.66), channel_id=1, source_target_pairs={{0,1},{1,0},{2,3},{3,2},{4,5},{5,4},{6,7},{7,6},{8,9},{9,8},{10,11... | collective-permute-start | bytes 16220168 | tf_op jit(solution)/shard_map/ppermute | solution.py:17
  261.5 3.5 copy-start.1
  261.5 3.5 copy-start.2
  267.8 276.7 %reduce-scatter.2.cloned.1.call-start = ((), (), s32[]{:S(2)}) async-start(), calls=%async_computation.3 | async-start | bytes 12582912 | tf_op jit(solution)/shard_map/reduce_scatter | solution.py:125
  304.5 6.3 slice-start
  305.9 5.0 slice-start.1
  305.9 5.0 slice-start.2
  310.9 2.4 copy-start.25
  310.9 2.4 copy-start.9
  313.4 3.0 copy-start.27
  316.3 3.0 copy-start.14
  316.3 3.0 copy-start.16
  334.1 200.6 %copy-start.5 = (bf16[128,2048]{1,0:T(8,128)(2,1)S(1)}, bf16[128,2048]{1,0:T(8,128)(2,1)}, u32[]{:S(2)}) copy-start(bf16[128,2048]{1,0:T(8,128)(2,1)} %param.7) | copy-start | bytes 1572868
  534.7 2.2 copy-start.24
  536.8 1.6 copy-start.11
  537.5 1.6 copy-start.6
  539.6 1.5 copy-start.10
  552.8 12.3 %copy-start.17 = (bf16[1280,384]{0,1:T(8,128)(2,1)S(1)}, bf16[1280,384]{0,1:T(8,128)(2,1)}, u32[]{:S(2)}) copy-start(bf16[1280,384]{0,1:T(8,128)(2,1)} %copy-done.16) | copy-start | bytes 2949124
  552.8 120.8 %all-to-all-start.1 = ((bf16[128,10,1152]{2,1,0:T(8,128)(2,1)}), bf16[128,10,1152]{2,1,0:T(8,128)(2,1)}, u32[]{:S(2)}, u32[]{:S(2)}) async-start(bf16[128,10,1152]{2,1,0:T(8,128)(2,1)} %copy.70), calls=%async_computation.2 | async-start | bytes 9437184 | tf_op jit(solution)/shard_map/all_to_all | solution.py:136
  565.2 6.7 copy-start.15
  571.8 6.7 copy-start.26
  571.8 6.7 copy-start.28
  684.0 4.3 copy-start.13
  684.0 4.6 copy-start.8
  684.0 4.6 copy-start.20
  684.0 4.6 copy-start.22
  (4 other events, 3.5 us)
Sparse Core Ops, SparseCore 0:
  268.0 266.6 all-reduce.5
Sparse Core Ops, SparseCore 1:
  334.2 16.1 reduce-scatter.1

commit v6 on v4

--- a/solution.py
+++ b/solution.py
@@ -128,19 +128,23 @@
         scatter_dimension=3,
         tiled=True,
     )
-    dot_back = jnp.broadcast_to(
-        dot_slot.astype(jnp.bfloat16).reshape(n_ha, n_dev, half, 1), (n_ha, n_dev, half, DOT_COLS)
-    )
-    ret = jnp.concatenate([input_half, dot_back], axis=3)
-    ret = jnp.transpose(ret, (1, 0, 2, 3)).reshape(n_dev, slot_count, feat + DOT_COLS)
+    dot_back = jnp.transpose(
+        dot_slot.astype(jnp.bfloat16).reshape(n_ha, n_dev, half), (1, 0, 2)
+    ).reshape(n_dev, slot_count)
+    ret = jnp.transpose(input_half, (1, 0, 2, 3)).reshape(n_dev, slot_count, feat)
     back = lax.all_to_all(ret, "de", split_axis=0, concat_axis=0, tiled=True)
-    back = back.reshape(total_slots, feat + DOT_COLS)[slot_of_route]
+    back_dots = lax.all_to_all(dot_back, "de", split_axis=0, concat_axis=0, tiled=True)
+    back = back.reshape(total_slots, feat)[slot_of_route]
     route_input = back[:, :feat].astype(jnp.float32)
     input_part = jnp.sum(route_input.reshape(tok_rows, route_count, feat), axis=1).astype(
         jnp.bfloat16
     )
     input_grad = lax.all_gather(input_part, "ha", axis=1, tiled=True)
-    route_dots = back[:, feat].astype(jnp.float32).reshape(tok_rows, route_count)
+    route_dots = (
+        back_dots.reshape(total_slots)[slot_of_route]
+        .astype(jnp.float32)
+        .reshape(tok_rows, route_count)
+    )
     dot_table = jnp.sum(
         jnp.where(routes[:, :, None] == expert_ids[None, None, :], route_dots[:, :, None], 0.0),
         axis=1,

time: 712 us -> 709 us (level)
  waiting for transfers between devices: 285 us -> 267 us
  starting transfers between devices: 12.5 us -> 23.1 us
  local copies, waits for them, and re-layouts: 107 us -> 116 us
    all_to_all x1, waiting for transfers between devices: 89 us -> 67.5 us  [layer(): back = lax.all_to_all(ret, 'de', split_axis=0, concat_axis=0, tiled=True)]
    all_to_all x0 -> x1, starting transfers between devices: none -> 11.4 us  [layer(): lax.all_to_all(dot_back, 'de', split_axis=0, concat_axis=0, tiled=True)]
  transfers between devices with their start and end apart: 4 -> 5, of which waited for: 2 -> 3; matrix products, arithmetic and copies ran while one was open for 14% -> 17% of each run, Pallas kernels for 0% -> 0%
where the time goes in v6:
time: 709 us; the launch traced here: 698 us
  waiting for transfers between devices  267 us (38%)
  blocking collectives  213 us (30%)
  local copies, waits for them, and re-layouts  116 us (16%)
  matrix products  42.6 us (6%)
  starting transfers between devices  23.1 us (3%)
  other arithmetic  19.5 us (3%)
  between operations  16.3 us (2%)
    all_to_all x1, blocking collectives, layer(): lax.all_to_all(send_xg, 'de', split_axis=0, concat_axis=0, tiled=True)  209 us
    psum x1, waiting for transfers between devices, spread(): return lax.psum(kept, axis)  196 us
    all_to_all x1, waiting for transfers between devices, layer(): back = lax.all_to_all(ret, 'de', split_axis=0, concat_axis=0, tiled=True)  67.5 us
    reshape x1, local copies, waits for them, and re-layouts, layer(): share_halves(recv_xg, core, n_ha).reshape(-1, 2 * model_width + DOT_COLS)  17.3 us
  transfers between devices with their start and end apart: 5, of which 3 were waited for; matrix products, arithmetic and copies ran while one was open for 17% of the time, Pallas kernels for 0%

profile of v6, /device:TPU:2, one launch (start us, length us, event | category | flops | bytes accessed | tf_op | source)
XLA Modules:
  0.0 698.2 jit_solution(679853806895265902)
XLA Ops:
  11.5 4.3 scatter_custom_fusion
  17.1 6.7 gather_fusion.5
  24.3 4.3 gather_fusion.2
  29.1 3.4 gather_fusion
  36.5 3.4 gather_fusion.1
  42.9 4.7 pad_maximum_fusion
  47.7 208.6 %all_to_all.19 = bf16[128,5,4224]{2,1,0:T(8,128)(2,1)S(1)} all-to-all(bf16[128,5,4224]{2,1,0:T(8,128)(2,1)S(1)} %pad_maximum_fusion), channel_id=1, replica_groups=mesh['de'=128,'ha'=2] {'de'}, dimensions={0} | all-to-all | bytes 10813440 | tf_op jit(solution)/shard_map/all_to_all | solution.py:116
  256.3 3.5 copy.70
  261.3 3.4 bitcast_select_fusion.5
  267.9 6.2 broadcast_in_dim.102
  274.0 8.0 %bitcast_dynamic-update-slice_fusion = bf16[2,128,5,4224]{3,2,1,0:T(8,128)(2,1)} fusion(bf16[2,128,5,4224]{3,2,1,0:T(8,128)(2,1)} %broadcast_in_dim.102, s32[]{:T(128)S(6)} %select_n.112, bf16[128,5,4224]{2,1,0:T(8,128)(2,1)} %copy-done), kind=kLoop, calls=%fused_computation.9 | loop fusion | bytes 17301508 | tf_op jit(solution)/shard_map/jit(dynamic_update_index_in_dim)/dynamic_update_slice | solution.py:19
  282.0 9.1 %copy_dynamic-update-slice_fusion = bf16[2,128,5,4224]{3,2,1,0:T(8,128)(2,1)} fusion(bf16[2,128,5,4224]{3,2,1,0:T(8,128)(2,1)} %bitcast_dynamic-update-slice_fusion, s32[]{:T(128)S(6)} %select_n.118, bf16[1,128,5,4224]{3,1,2,0:T(8,128)(2,1)} %bitcast.8), kind=kLoop, calls=%fused_computation.10 | loop fusion | bytes 14057476 | tf_op jit(solution)/shard_map/jit(dynamic_update_index_in_dim)/dynamic_update_slice | solution.py:20
  291.1 17.3 %reshape.229 = bf16[1280,4224]{1,0:T(8,128)(2,1)} reshape(bf16[2,128,5,4224]{3,2,1,0:T(8,128)(2,1)} %copy_dynamic-update-slice_fusion) | data formatting | bytes 21626880 | tf_op jit(solution)/shard_map/reshape | solution.py:117
  309.8 5.0 fusion.10
  317.3 3.0 multiply_reduce_fusion
  320.3 2.9 fusion.31
  323.3 4.8 add_convert_fusion
  328.1 10.2 %convert_element_type.68 = bf16[2,128,5,2048]{3,2,1,0:T(8,128)(2,1)} reshape(bf16[1280,2048]{1,0:T(8,128)(2,1)} %add_convert_fusion) | data formatting | bytes 10485760 | tf_op jit(solution)/shard_map/convert_element_type | solution.py:126
  338.3 196.2 %all-reduce.6.cloned.1.call-done = (bf16[2048,384]{1,0:T(8,128)(2,1)}, bf16[2048,384]{1,0:T(8,128)(2,1)}, bf16[384,2048]{1,0:T(8,128)(2,1)}, bf16[2048,384]{1,0:...) async-done(((bf16[2048,384]{1,0:T(8,128)(2,1)}, bf16[2048,384]{1,0:T(8,128)(2,1)}, bf16[384,2048]{1,0:T(8,128)(2,1)}, bf16[2048,384]{1,0:T(8,128)(2,1)}, ...) | async-done | bytes 9437200 | tf_op jit(solution)/shard_map/psum | solution.py:13
  545.2 11.4 %all-to-all-start.2 = ((bf16[128,1,10]{2,1,0:T(2,128)(2,1)}), bf16[128,1,10]{2,1,0:T(2,128)(2,1)S(1)}, u32[]{:S(2)}, u32[]{:S(2)}) async-start(bf16[128,1,10]{2,1,0:T(2,128)(2,1)} %copy.76), calls=%async_computation.3 | async-start | bytes 131072 | tf_op jit(solution)/shard_map/all_to_all | solution.py:136
  556.6 3.9 copy.72
  560.5 3.6 copy.73
  564.1 3.3 all-to-all-done.2
  567.4 11.5 %all-to-all-start.1 = ((bf16[128,10,1024]{2,1,0:T(8,128)(2,1)}), bf16[128,10,1024]{2,1,0:T(8,128)(2,1)}, u32[]{:S(2)}, u32[]{:S(2)}) async-start(bf16[128,10,1024]{2,1,0:T(8,128)(2,1)} %copy.73), calls=%async_computation.2 | async-start | bytes 8388608 | tf_op jit(solution)/shard_map/all_to_all | solution.py:135
  578.9 6.7 fusion.24
  585.6 6.7 fusion.27
  592.3 6.0 fusion.21
  598.6 6.8 gather_fusion.4
  606.9 67.5 %all-to-all-done.1 = bf16[128,10,1024]{2,1,0:T(8,128)(2,1)} async-done(((bf16[128,10,1024]{2,1,0:T(8,128)(2,1)}), bf16[128,10,1024]{2,1,0:T(8,128)(2,1)}, u32[]{:S(2)}, u32[]{:S(2)}) %all-to-all-start.1) | async-done | bytes 2621472 | tf_op jit(solution)/shard_map/all_to_all | solution.py:135
  674.4 4.8 reshape.231
  679.2 5.4 gather_fusion.3
  684.6 3.0 bitcast_reduce_fusion
  (126 shorter events, 36.4 us)
Async XLA Ops:
  8.0 526.5 %all-reduce.6.cloned.1.call-start = ((), (), s32[]{:S(2)}) async-start(), calls=%async_computation.5 | async-start | bytes 18874368 | tf_op jit(solution)/shard_map/psum | solution.py:13
  10.5 5.9 copy-start.7
  17.1 6.9 copy-start.15
  24.3 4.8 copy-start.4
  256.3 5.0 copy-start
  261.3 20.7 %collective-permute-start = (bf16[128,5,4224]{2,0,1:T(8,128)(2,1)}, bf16[128,5,4224]{2,0,1:T(8,128)(2,1)}, u32[]{:S(2)}, u32[]{:S(2)}) collective-permute-start(bf16[128,5,4224]{2,0,1:T(8,128)(2,1)} %copy.70), channel_id=1, source_target_pairs={{0,1},{1,0},{2,3},{3,2},{4,5},{5,4},{6,7},{7,6},{8,9},{9,8},{10,11... | collective-permute-start | bytes 16220168 | tf_op jit(solution)/shard_map/ppermute | solution.py:17
  261.3 3.4 copy-start.1
  261.3 3.4 copy-start.2
  267.6 289.0 %reduce-scatter.2.cloned.1.call-start = ((), (), s32[]{:S(2)}) async-start(), calls=%async_computation.4 | async-start | bytes 12582912 | tf_op jit(solution)/shard_map/reduce_scatter | solution.py:125
  308.4 6.3 slice-start
  309.7 5.0 slice-start.1
  309.7 5.1 slice-start.2
  314.9 2.4 copy-start.18
  314.9 2.4 copy-start.8
  317.3 3.0 copy-start.20
  320.3 3.0 copy-start.11
  320.3 3.0 copy-start.13
  338.3 196.2 %copy-start.5 = (bf16[128,2048]{1,0:T(8,128)(2,1)S(1)}, bf16[128,2048]{1,0:T(8,128)(2,1)}, u32[]{:S(2)}) copy-start(bf16[128,2048]{1,0:T(8,128)(2,1)} %param.7) | copy-start | bytes 1572868
  534.5 2.2 copy-start.17
  536.6 1.0 copy-start.3
  536.6 1.6 copy-start.10
  537.3 1.6 copy-start.6
  538.8 1.4 copy-start.16
  539.4 1.5 copy-start.9
  545.2 22.2 %all-to-all-start.2 = ((bf16[128,1,10]{2,1,0:T(2,128)(2,1)}), bf16[128,1,10]{2,1,0:T(2,128)(2,1)S(1)}, u32[]{:S(2)}, u32[]{:S(2)}) async-start(bf16[128,1,10]{2,1,0:T(2,128)(2,1)} %copy.76), calls=%async_computation.3 | async-start | bytes 131072 | tf_op jit(solution)/shard_map/all_to_all | solution.py:136
  564.1 14.8 %copy-start.14 = (bf16[1280,384]{0,1:T(8,128)(2,1)S(1)}, bf16[1280,384]{0,1:T(8,128)(2,1)}, u32[]{:S(2)}) copy-start(bf16[1280,384]{0,1:T(8,128)(2,1)} %copy-done.13) | copy-start | bytes 2949124
  567.4 107.0 %all-to-all-start.1 = ((bf16[128,10,1024]{2,1,0:T(8,128)(2,1)}), bf16[128,10,1024]{2,1,0:T(8,128)(2,1)}, u32[]{:S(2)}, u32[]{:S(2)}) async-start(bf16[128,10,1024]{2,1,0:T(8,128)(2,1)} %copy.73), calls=%async_computation.2 | async-start | bytes 8388608 | tf_op jit(solution)/shard_map/all_to_all | solution.py:135
  578.9 6.7 copy-start.12
  585.6 6.7 copy-start.19
  585.6 6.7 copy-start.21
Sparse Core Ops, SparseCore 0:
  267.8 266.6 all-reduce.5
Sparse Core Ops, SparseCore 1:
  338.4 16.9 reduce-scatter.1
